TPU v7x, 32 devices: a whole 2x2x4 slice. The times are simulated.
32 devices in a mesh: heads: 2 (over x), blk: 16 (over z, y, core).
Axes of the slice: x: 2, y: 2, z: 4, core: 2. Of those that a mesh axis runs over, the one named last changes fastest.
Arguments:
- queries: bfloat16 [1024, 64, 128], P('blk', 'heads'), may hold values from -8 to 8
- prefix_keys: bfloat16 [8, 32768, 128], P('heads', 'blk'), may hold values from -8 to 8
- cached_prefix_values: bfloat16 [8, 32768, 128], P('heads', 'blk'), may hold values from -6 to 6
- shard_len: int32 [16], replicated, may hold values from 512 to 2048
- reach: int32 [16], replicated, may hold values from 4096 to 8192
- w_out: bfloat16 [8192, 16384], P('heads', 'blk'), may hold values from -0.0625 to 0.0625
Outputs:
- projected: bfloat16 [1024, 16384], P('heads', 'blk')
All inputs are finite; a program needn't handle non-finite values.
Results may differ from a plain program's by a relative error of at most 0.0056.
Values may be sent and summed in bfloat16 or wider, within the bound.
A program may use at most 128 MiB of HBM per device.

v0:
```python
import jax
import jax.numpy as jnp
from jax import lax
from jax.sharding import PartitionSpec as P

SPAN = 4


masked_score = -1e30


def passed_along(value, axis, steps):
    count = lax.axis_size(axis)
    pairs = [(source, (source + steps) % count) for source in range(count)]
    return lax.ppermute(value, axis, pairs)


def part_stats(query_tile_rows, key_block, value_block, visible):
    head_size = query_tile_rows.shape[-1]
    scores = jnp.einsum(
        "thgd,hnd->thgn", query_tile_rows, key_block, preferred_element_type=jnp.float32
    ) * head_size ** (-0.5)
    visible_grid = visible[:, None, None, :]
    maxima = jnp.max(jnp.where(visible_grid, scores, masked_score), axis=-1)
    weights = jnp.where(visible_grid, jnp.exp(scores - maxima[..., None]), 0.0)
    totals = jnp.sum(weights, axis=-1)
    weighted = jnp.einsum(
        "thgn,hnd->thgd",
        weights.astype(jnp.bfloat16),
        value_block,
        preferred_element_type=jnp.float32,
    )
    return (maxima, totals, weighted)


def combine_parts(first, second):
    joined = jnp.maximum(first[0], second[0])
    first_factor = jnp.exp(first[0] - joined)
    second_factor = jnp.exp(second[0] - joined)
    totals = first[1] * first_factor + second[1] * second_factor
    weighted = first[2] * first_factor[..., None] + second[2] * second_factor[..., None]
    return (joined, totals, weighted)


def on_device(queries, prefix_keys, cached_prefix_values, shard_len, reach, w_out):
    shard_count = lax.axis_size("blk")
    own_index = lax.axis_index("blk")
    query_len = queries.shape[0]
    heads_local = queries.shape[1]
    head_size = queries.shape[2]
    kv_local = prefix_keys.shape[0]
    keys_len = prefix_keys.shape[1]
    local_queries = queries.reshape(query_len, kv_local, heads_local // kv_local, head_size)
    row_ids = jnp.arange(query_len, dtype=jnp.int32)[:, None]
    slot_ids = jnp.arange(keys_len, dtype=jnp.int32)[None, :]

    def mask_for(block_id, shard_id, offset):
        return (slot_ids < shard_len[shard_id]) & (
            offset * keys_len + slot_ids < reach[block_id] + row_ids
        )

    running = part_stats(
        local_queries, prefix_keys, cached_prefix_values, mask_for(own_index, own_index, 0)
    )
    for offset in range(1, SPAN):
        visitor = passed_along(local_queries, "blk", offset)
        owner_id = (own_index - offset + shard_count) % shard_count
        maxima, totals, weighted = part_stats(
            visitor, prefix_keys, cached_prefix_values, mask_for(owner_id, own_index, offset)
        )
        returned = passed_along((maxima, totals, weighted), "blk", -offset)
        running = combine_parts(running, returned)
    attended = (
        (running[2] / running[1][..., None])
        .astype(jnp.bfloat16)
        .reshape(query_len, heads_local * head_size)
    )
    partial_out = jnp.dot(
        lax.all_gather(attended, "blk", axis=0, tiled=True),
        w_out,
        preferred_element_type=jnp.float32,
    )
    return lax.psum_scatter(partial_out, "heads", scatter_dimension=0, tiled=True).astype(
        jnp.bfloat16
    )


def solution(mesh):
    return jax.shard_map(
        on_device,
        mesh=mesh,
        in_specs=(
            P("blk", "heads", None),
            P("heads", "blk", None),
            P("heads", "blk", None),
            P(),
            P(),
            P("heads", "blk"),
        ),
        out_specs=P("heads", "blk"),
        check_vma=False,
    )
```

profile of v0, /device:TPU:14, one launch (start us, length us, event | category | flops | bytes accessed | tf_op | source)
XLA Modules:
  0.0 335.5 jit_solution(10008694626200140312)
XLA Ops:
  6.5 1.4 copy.19
  8.9 1.5 collective-permute-start.3
  12.9 1.5 fusion.64
  14.4 1.3 iota_add_fusion.5
  15.7 1.2 iota_add_fusion.3
  17.4 7.2 %fusion.9 = (f32[64,4,8]{0,2,1:T(8,128)S(1)}, f32[4,2048,64,8]{1,2,3,0:T(8,128)}) fusion(pred[64,2048]{1,0:T(8,128)(4,1)S(1)} %get-tuple-element.12, bf16[64,4,8,128]{3,0,2,1:T(8,128)(2,1)S(1)} %bitcast.131, bf16[4,2048,128]{2,1,0:T(8,128)(2,1)S(1)} %copy-done), kind=kOutput, calls=%fused_computation.17 | convolution fusion | flops 1086322688 | bytes 19537920 | tf_op jit(solution)/shard_map/thgd,hnd->thgn/dot_general | solution.py:20
  24.6 9.6 %fusion.26 = f32[4,64,8,128]{3,1,2,0:T(8,128)} fusion(f32[4,2048,64,8]{1,2,3,0:T(8,128)} %get-tuple-element.27, f32[64,4,8]{0,2,1:T(8,128)S(1)} %get-tuple-element.26, pred[64,2048]{1,0:T(8,128)(4,1)S(1)} %get-tuple-element.12, bf16[4,2048,128]{2,1,0:T(8,128)(2,1)S(1)} %copy-done.2), kind=kOutput, calls=%fused_computation.31 | convolution fusion | flops 1090519040 | bytes 20062208 | tf_op jit(solution)/shard_map/thgn,hnd->thgd/dot_general | solution.py:27
  34.2 8.3 %fusion.6 = (f32[64,4,8]{0,2,1:T(8,128)S(1)}, f32[4,2048,64,8]{1,2,3,0:T(8,128)}) fusion(pred[64,2048]{1,0:T(8,128)(4,1)S(1)} %get-tuple-element.13, bf16[64,4,8,128]{3,0,2,1:T(8,128)(2,1)} %collective-permute-done, bf16[4,2048,128]{2,1,0:T(8,128)(2,1)S(1)} %copy-done), kind=kOutput, calls=%fused_computation.12 | convolution fusion | flops 1086322688 | bytes 19537920 | tf_op jit(solution)/shard_map/thgd,hnd->thgn/dot_general | solution.py:20
  42.4 8.0 %fusion.24 = f32[4,64,8,128]{3,1,2,0:T(8,128)S(1)} fusion(f32[4,2048,64,8]{1,2,3,0:T(8,128)} %get-tuple-element.25, f32[64,4,8]{0,2,1:T(8,128)S(1)} %get-tuple-element.24, pred[64,2048]{1,0:T(8,128)(4,1)S(1)} %get-tuple-element.13, bf16[4,2048,128]{2,1,0:T(8,128)(2,1)S(1)} %copy-done.2), kind=kOutput, calls=%fused_computation.30 | convolution fusion | flops 1090519040 | bytes 20062208 | tf_op jit(solution)/shard_map/thgn,hnd->thgd/dot_general | solution.py:27
  50.4 8.1 %fusion.14 = f32[64,4,8]{0,2,1:T(8,128)S(1)} fusion(f32[4,2048,64,8]{1,2,3,0:T(8,128)} %get-tuple-element.25, f32[64,4,8]{0,2,1:T(8,128)S(1)} %get-tuple-element.24, pred[64,2048]{1,0:T(8,128)(4,1)S(1)} %get-tuple-element.13), kind=kLoop, calls=%fused_computation.22 | loop fusion | flops 16775168 | bytes 16924672 | tf_op jit(solution)/shard_map/reduce_sum | solution.py:26
  58.5 1.5 collective-permute-start.1
  60.1 8.3 %fusion.3 = (f32[64,4,8]{0,2,1:T(8,128)S(1)}, f32[4,2048,64,8]{1,2,3,0:T(8,128)}) fusion(pred[64,2048]{1,0:T(8,128)(4,1)S(1)} %get-tuple-element.14, bf16[64,4,8,128]{3,0,2,1:T(8,128)(2,1)} %collective-permute-done.3, bf16[4,2048,128]{2,1,0:T(8,128)(2,1)S(1)} %copy-done), kind=kOutput, calls=%fused_computation.7 | convolution fusion | flops 1086322688 | bytes 19537920 | tf_op jit(solution)/shard_map/thgd,hnd->thgn/dot_general | solution.py:20
  68.3 8.0 %fusion.22 = f32[4,64,8,128]{3,1,2,0:T(8,128)S(1)} fusion(f32[4,2048,64,8]{1,2,3,0:T(8,128)} %get-tuple-element.23, f32[64,4,8]{0,2,1:T(8,128)S(1)} %get-tuple-element.22, pred[64,2048]{1,0:T(8,128)(4,1)S(1)} %get-tuple-element.14, bf16[4,2048,128]{2,1,0:T(8,128)(2,1)S(1)} %copy-done.2), kind=kOutput, calls=%fused_computation.29 | convolution fusion | flops 1090519040 | bytes 20062208 | tf_op jit(solution)/shard_map/thgn,hnd->thgd/dot_general | solution.py:27
  76.3 8.1 %fusion.16 = f32[64,4,8]{0,2,1:T(8,128)S(1)} fusion(f32[4,2048,64,8]{1,2,3,0:T(8,128)} %get-tuple-element.23, f32[64,4,8]{0,2,1:T(8,128)S(1)} %get-tuple-element.22, pred[64,2048]{1,0:T(8,128)(4,1)S(1)} %get-tuple-element.14), kind=kLoop, calls=%fused_computation.24 | loop fusion | flops 16775168 | bytes 16924672 | tf_op jit(solution)/shard_map/reduce_sum | solution.py:26
  84.4 5.2 %collective-permute-start.4 = (f32[64,4,8]{0,2,1:T(8,128)S(1)}, f32[64,4,8]{0,2,1:T(8,128)S(1)}, u32[]{:S(2)}, u32[]{:S(2)}) collective-permute-start(f32[64,4,8]{0,2,1:T(8,128)S(1)} %get-tuple-element.22), channel_id=1, source_target_pairs={{0,14},{1,15},{2,0},{3,1},{4,2},{5,3},{6,4},{7,5},{8,6},{9,7},{10,... | collective-permute-start | bytes 24584 | tf_op jit(solution)/shard_map/ppermute | solution.py:15
  89.8 3.4 %collective-permute-start.10 = (f32[64,4,8]{0,2,1:T(8,128)S(1)}, f32[64,4,8]{0,2,1:T(8,128)S(1)}, u32[]{:S(2)}, u32[]{:S(2)}) collective-permute-start(f32[64,4,8]{0,2,1:T(8,128)S(1)} %fusion.16), channel_id=1, source_target_pairs={{0,14},{1,15},{2,0},{3,1},{4,2},{5,3},{6,4},{7,5},{8,6},{9,7},{10,... | collective-permute-start | bytes 24584 | tf_op jit(solution)/shard_map/ppermute | solution.py:15
  93.2 7.2 %fusion = (f32[64,4,8]{0,2,1:T(8,128)S(1)}, f32[4,2048,64,8]{1,2,3,0:T(8,128)}) fusion(pred[64,2048]{1,0:T(8,128)(4,1)S(1)} %get-tuple-element.15, bf16[64,4,8,128]{3,0,2,1:T(8,128)(2,1)S(1)} %collective-permute-done.6, bf16[4,2048,128]{2,1,0:T(8,128)(2,1)S(1)} %copy-done), kind=kOutput, calls=%fused_computation.2 | convolution fusion | flops 1086322688 | bytes 19537920 | tf_op jit(solution)/shard_map/thgd,hnd->thgn/dot_general | solution.py:20
  100.4 8.0 %fusion.20 = f32[4,64,8,128]{3,1,2,0:T(8,128)S(1)} fusion(f32[4,2048,64,8]{1,2,3,0:T(8,128)} %get-tuple-element.21, f32[64,4,8]{0,2,1:T(8,128)S(1)} %get-tuple-element.20, pred[64,2048]{1,0:T(8,128)(4,1)S(1)} %get-tuple-element.15, bf16[4,2048,128]{2,1,0:T(8,128)(2,1)S(1)} %copy-done.2), kind=kOutput, calls=%fused_computation.28 | convolution fusion | flops 1090519040 | bytes 20062208 | tf_op jit(solution)/shard_map/thgn,hnd->thgd/dot_general | solution.py:27
  108.4 8.1 %fusion.18 = f32[64,4,8]{0,2,1:T(8,128)S(1)} fusion(f32[4,2048,64,8]{1,2,3,0:T(8,128)} %get-tuple-element.21, f32[64,4,8]{0,2,1:T(8,128)S(1)} %get-tuple-element.20, pred[64,2048]{1,0:T(8,128)(4,1)S(1)} %get-tuple-element.15), kind=kLoop, calls=%fused_computation.26 | loop fusion | flops 16775168 | bytes 16924672 | tf_op jit(solution)/shard_map/reduce_sum | solution.py:26
  118.4 3.0 collective-permute-start.2
  121.7 1.7 collective-permute-start.8
  123.5 8.1 %fusion.12 = f32[64,4,8]{0,2,1:T(8,128)S(1)} fusion(f32[4,2048,64,8]{1,2,3,0:T(8,128)} %get-tuple-element.27, f32[64,4,8]{0,2,1:T(8,128)S(1)} %get-tuple-element.26, pred[64,2048]{1,0:T(8,128)(4,1)S(1)} %get-tuple-element.12), kind=kLoop, calls=%fused_computation.20 | loop fusion | flops 16775168 | bytes 16924672 | tf_op jit(solution)/shard_map/reduce_sum | solution.py:26
  131.6 13.2 %collective-permute-done.11 = f32[64,4,8]{0,2,1:T(8,128)S(1)} collective-permute-done((f32[64,4,8]{0,2,1:T(8,128)S(1)}, f32[64,4,8]{0,2,1:T(8,128)S(1)}, u32[]{:S(2)}, u32[]{:S(2)}) %collective-permute-start.11) | collective-permute-done | bytes 8224 | tf_op jit(solution)/shard_map/ppermute | solution.py:15
  146.4 1.5 copy.24
  147.9 1.5 copy.26
  149.4 1.5 copy.27
  151.6 16.1 %collective-permute-done.5 = f32[64,4,8,128]{3,2,0,1:T(8,128)} collective-permute-done((f32[64,4,8,128]{3,2,0,1:T(8,128)S(1)}, f32[64,4,8,128]{3,2,0,1:T(8,128)}, u32[]{:S(2)}, u32[]{:S(2)}) %collective-permute-start.5) | collective-permute-done | bytes 1048608 | tf_op jit(solution)/shard_map/ppermute | solution.py:15
  167.7 4.2 %fusion.50 = bf16[64,4,8,128]{3,2,0,1:T(8,128)(2,1)S(1)} fusion(f32[64,4,8,128]{3,2,0,1:T(8,128)} %collective-permute-done.8, f32[64,4,8,128]{3,2,0,1:T(8,128)} %collective-permute-done.5, f32[64,4,8,128]{3,2,0,1:T(8,128)} %collective-permute-done.2, f32[4,64,8,128]{3,1,2,0:T(8,128)} %fusion.26, f32[64,4,8]{2,0,1:T(8,128)S(1)} %copy.30, ...), kind=kLoop, calls=%fused_computation.58 | loop fusion | flops 2883584 | bytes 4775936 | tf_op jit(solution)/shard_map/convert_element_type | solution.py:75
  173.1 84.2 %all-gather.2.cloned.1.call-done = bf16[1024,4096]{1,0:T(8,128)(2,1)} async-done(((bf16[64,4096]{1,0:T(8,128)(2,1)}), bf16[1024,4096]{1,0:T(8,128)(2,1)}) %all-gather.2.cloned.1.call-update) | async-done | bytes 8388624 | tf_op jit(solution)/shard_map/all_gather | solution.py:79
  257.3 15.2 %fusion.65 = f32[1024,1024]{1,0:T(8,128)} fusion(bf16[1024,4096]{1,0:T(8,128)(2,1)} %all-gather.2.cloned.1.call-done, bf16[4096,1024]{1,0:T(8,128)(2,1)} %param.11), kind=kOutput, calls=%fused_computation.91 | convolution fusion | flops 8589934592 | bytes 20971520 | tf_op jit(solution)/shard_map/dot_general | solution.py:78
  272.6 53.3 %reduce-scatter.2.cloned.1.call-done = f32[512,1024]{1,0:T(8,128)} async-done(((f32[1024,1024]{1,0:T(8,128)}), f32[512,1024]{1,0:T(8,128)}) %reduce-scatter.2.cloned.1.call-update) | async-done | bytes 2097168 | tf_op jit(solution)/shard_map/reduce_scatter | solution.py:83
  325.9 2.7 convert_element_type.23
  (41 shorter events, 9.7 us)
Async XLA Ops:
  6.5 10.8 %copy-start = (bf16[4,2048,128]{2,1,0:T(8,128)(2,1)S(1)}, bf16[4,2048,128]{2,1,0:T(8,128)(2,1)}, u32[]{:S(2)}) copy-start(bf16[4,2048,128]{2,1,0:T(8,128)(2,1)} %param.7) | copy-start | bytes 6291460
  6.5 250.8 %all-gather.2.cloned.1.call-start = ((), (), s32[]{:S(2)}) async-start(), calls=%async_computation.1 | async-start | bytes 8912896 | tf_op jit(solution)/shard_map/all_gather | solution.py:79
  7.9 85.3 %collective-permute-start.6 = (bf16[64,4,8,128]{3,0,2,1:T(8,128)(2,1)S(1)}, bf16[64,4,8,128]{3,0,2,1:T(8,128)(2,1)S(1)}, u32[]{:S(2)}, u32[]{:S(2)}) collective-permute-start(bf16[64,4,8,128]{3,0,2,1:T(8,128)(2,1)S(1)} %bitcast.128), channel_id=1, source_target_pairs={{0,3},{1,4},{2,5},{3,6},{4,7},{5,8},{6,9},{7,10},{8,11},{9,12},{10... | collective-permute-start | bytes 1572872 | tf_op jit(solution)/shard_map/ppermute | solution.py:15
  8.9 51.1 %collective-permute-start.3 = (bf16[64,4,8,128]{3,0,2,1:T(8,128)(2,1)S(1)}, bf16[64,4,8,128]{3,0,2,1:T(8,128)(2,1)}, u32[]{:S(2)}, u32[]{:S(2)}) collective-permute-start(bf16[64,4,8,128]{3,0,2,1:T(8,128)(2,1)S(1)} %bitcast.129), channel_id=1, source_target_pairs={{0,2},{1,3},{2,4},{3,5},{4,6},{5,7},{6,8},{7,9},{8,10},{9,11},{10,... | collective-permute-start | bytes 1572872 | tf_op jit(solution)/shard_map/ppermute | solution.py:15
  10.5 23.7 %collective-permute-start = (bf16[64,4,8,128]{3,0,2,1:T(8,128)(2,1)S(1)}, bf16[64,4,8,128]{3,0,2,1:T(8,128)(2,1)}, u32[]{:S(2)}, u32[]{:S(2)}) collective-permute-start(bf16[64,4,8,128]{3,0,2,1:T(8,128)(2,1)S(1)} %bitcast.130), channel_id=1, source_target_pairs={{0,1},{1,2},{2,3},{3,4},{4,5},{5,6},{6,7},{7,8},{8,9},{9,10},{10,1... | collective-permute-start | bytes 1572872 | tf_op jit(solution)/shard_map/ppermute | solution.py:15
  12.8 11.7 %copy-start.2 = (bf16[4,2048,128]{2,1,0:T(8,128)(2,1)S(1)}, bf16[4,2048,128]{2,1,0:T(8,128)(2,1)}, u32[]{:S(2)}) copy-start(bf16[4,2048,128]{2,1,0:T(8,128)(2,1)} %param.8) | copy-start | bytes 6291460
  58.5 62.8 %collective-permute-start.1 = (f32[64,4,8]{0,2,1:T(8,128)S(1)}, f32[64,4,8]{0,2,1:T(8,128)S(1)}, u32[]{:S(2)}, u32[]{:S(2)}) collective-permute-start(f32[64,4,8]{0,2,1:T(8,128)S(1)} %get-tuple-element.24), channel_id=1, source_target_pairs={{0,15},{1,0},{2,1},{3,2},{4,3},{5,4},{6,5},{7,6},{8,7},{9,8},{10,9... | collective-permute-start | bytes 24584 | tf_op jit(solution)/shard_map/ppermute | solution.py:15
  84.4 37.3 %collective-permute-start.4 = (f32[64,4,8]{0,2,1:T(8,128)S(1)}, f32[64,4,8]{0,2,1:T(8,128)S(1)}, u32[]{:S(2)}, u32[]{:S(2)}) collective-permute-start(f32[64,4,8]{0,2,1:T(8,128)S(1)} %get-tuple-element.22), channel_id=1, source_target_pairs={{0,14},{1,15},{2,0},{3,1},{4,2},{5,3},{6,4},{7,5},{8,6},{9,7},{10,... | collective-permute-start | bytes 24584 | tf_op jit(solution)/shard_map/ppermute | solution.py:15
  89.6 28.7 %collective-permute-start.9 = (f32[64,4,8]{0,2,1:T(8,128)S(1)}, f32[64,4,8]{0,2,1:T(8,128)S(1)}, u32[]{:S(2)}, u32[]{:S(2)}) collective-permute-start(f32[64,4,8]{0,2,1:T(8,128)S(1)} %fusion.14), channel_id=1, source_target_pairs={{0,15},{1,0},{2,1},{3,2},{4,3},{5,4},{6,5},{7,6},{8,7},{9,8},{10,9... | collective-permute-start | bytes 24584 | tf_op jit(solution)/shard_map/ppermute | solution.py:15
  89.8 31.9 %collective-permute-start.10 = (f32[64,4,8]{0,2,1:T(8,128)S(1)}, f32[64,4,8]{0,2,1:T(8,128)S(1)}, u32[]{:S(2)}, u32[]{:S(2)}) collective-permute-start(f32[64,4,8]{0,2,1:T(8,128)S(1)} %fusion.16), channel_id=1, source_target_pairs={{0,14},{1,15},{2,0},{3,1},{4,2},{5,3},{6,4},{7,5},{8,6},{9,7},{10,... | collective-permute-start | bytes 24584 | tf_op jit(solution)/shard_map/ppermute | solution.py:15
  116.5 28.3 %collective-permute-start.7 = (f32[64,4,8]{0,2,1:T(8,128)S(1)}, f32[64,4,8]{0,2,1:T(8,128)S(1)}, u32[]{:S(2)}, u32[]{:S(2)}) collective-permute-start(f32[64,4,8]{0,2,1:T(8,128)S(1)} %get-tuple-element.20), channel_id=1, source_target_pairs={{0,13},{1,14},{2,15},{3,0},{4,1},{5,2},{6,3},{7,4},{8,5},{9,6},{10... | collective-permute-start | bytes 24584 | tf_op jit(solution)/shard_map/ppermute | solution.py:15
  118.4 33.2 %collective-permute-start.2 = (f32[64,4,8,128]{3,2,0,1:T(8,128)S(1)}, f32[64,4,8,128]{3,2,0,1:T(8,128)}, u32[]{:S(2)}, u32[]{:S(2)}) collective-permute-start(f32[64,4,8,128]{3,2,0,1:T(8,128)S(1)} %bitcast.136), channel_id=1, source_target_pairs={{0,15},{1,0},{2,1},{3,2},{4,3},{5,4},{6,5},{7,6},{8,7},{9,8},{10,9... | collective-permute-start | bytes 3145736 | tf_op jit(solution)/shard_map/ppermute | solution.py:15
  121.4 46.3 %collective-permute-start.5 = (f32[64,4,8,128]{3,2,0,1:T(8,128)S(1)}, f32[64,4,8,128]{3,2,0,1:T(8,128)}, u32[]{:S(2)}, u32[]{:S(2)}) collective-permute-start(f32[64,4,8,128]{3,2,0,1:T(8,128)S(1)} %bitcast.135), channel_id=1, source_target_pairs={{0,14},{1,15},{2,0},{3,1},{4,2},{5,3},{6,4},{7,5},{8,6},{9,7},{10,... | collective-permute-start | bytes 3145736 | tf_op jit(solution)/shard_map/ppermute | solution.py:15
  121.7 23.1 %collective-permute-start.11 = (f32[64,4,8]{0,2,1:T(8,128)S(1)}, f32[64,4,8]{0,2,1:T(8,128)S(1)}, u32[]{:S(2)}, u32[]{:S(2)}) collective-permute-start(f32[64,4,8]{0,2,1:T(8,128)S(1)} %fusion.18), channel_id=1, source_target_pairs={{0,13},{1,14},{2,15},{3,0},{4,1},{5,2},{6,3},{7,4},{8,5},{9,6},{10... | collective-permute-start | bytes 24584 | tf_op jit(solution)/shard_map/ppermute | solution.py:15
  121.7 46.0 %collective-permute-start.8 = (f32[64,4,8,128]{3,2,0,1:T(8,128)S(1)}, f32[64,4,8,128]{3,2,0,1:T(8,128)}, u32[]{:S(2)}, u32[]{:S(2)}) collective-permute-start(f32[64,4,8,128]{3,2,0,1:T(8,128)S(1)} %bitcast.134), channel_id=1, source_target_pairs={{0,13},{1,14},{2,15},{3,0},{4,1},{5,2},{6,3},{7,4},{8,5},{9,6},{10... | collective-permute-start | bytes 3145736 | tf_op jit(solution)/shard_map/ppermute | solution.py:15
  173.0 152.9 %reduce-scatter.2.cloned.1.call-start = ((), (), s32[]{:S(2)}) async-start(), calls=%async_computation.2 | async-start | bytes 6291456 | tf_op jit(solution)/shard_map/reduce_scatter | solution.py:83
  257.3 71.3 %copy-start.1 = (bf16[4,2048,128]{2,1,0:T(8,128)(2,1)S(1)}, bf16[4,2048,128]{2,1,0:T(8,128)(2,1)}, u32[]{:S(2)}) copy-start(bf16[4,2048,128]{2,1,0:T(8,128)(2,1)} %param.7) | copy-start | bytes 6291460
Sparse Core Ops, SparseCore 0:
  173.2 84.1 all-gather.1
  272.7 53.1 reduce-scatter.1
where the time goes:
time: 339 us; the launch traced here: 335 us
  waiting for transfers between devices  167 us (49%)
  matrix products  79.7 us (24%)
  other arithmetic  43.7 us (13%)
  starting transfers between devices  18.4 us (5%)
  between operations  13.6 us (4%)
  local copies, waits for them, and re-layouts  13.3 us (4%)
    all_gather x1, waiting for transfers between devices, on_device(): lax.all_gather(attended, 'blk', axis=0, tiled=True)  84.2 us
    reduce_scatter x1, waiting for transfers between devices, on_device(): lax.psum_scatter(partial_out, 'heads', scatter_dimension=0, tiled=True)  53.3 us
    dot_general x4, matrix products, part_stats(): jnp.einsum('thgn,hnd->thgd', weights.astype(jnp.bfloat16), value_block, p...  33.5 us
    reduce_sum x4, other arithmetic, part_stats(): totals = jnp.sum(weights, axis=-1)  32.5 us
    dot_general x4, matrix products, part_stats(): jnp.einsum('thgd,hnd->thgn', query_tile_rows, key_block, preferred_elemen...  30.9 us
    ppermute x12, waiting for transfers between devices, passed_along(): return lax.ppermute(value, axis, pairs)  29.3 us
    ppermute x12, starting transfers between devices, passed_along(): return lax.ppermute(value, axis, pairs)  18.3 us
    dot_general x1, matrix products, on_device(): jnp.dot(lax.all_gather(attended, 'blk', axis=0, tiled=True), w_out, prefe...  15.2 us
  transfers between devices with their start and end apart: 14, of which 4 were waited for; matrix products, arithmetic and copies ran while one was open for 33% of the time, Pallas kernels for 0%

commit v1 on v0

v1 whole, which is shorter than its diff:
```python
import functools
import math

import jax
import jax.numpy as jnp
from jax import lax
from jax.experimental import pallas as pl
from jax.experimental.pallas import tpu as pltpu
from jax.sharding import PartitionSpec as P

SPAN = 4
LANES = 128
masked_score = -1e30


def passed_along(value, axis, steps):
    count = lax.axis_size(axis)
    pairs = [(source, (source + steps) % count) for source in range(count)]
    return lax.ppermute(value, axis, pairs)


def attend_kernel(tile, group, head_size, bounds, q_ref, k_ref, v_ref, o_ref, s_ref, q_all, m_ref, l_ref, acc_ref):
    rows = q_ref.shape[0]
    keys = k_ref.shape[1]
    kv = pl.program_id(0)
    live, edge = bounds[0], bounds[1]
    factor = head_size**-0.5 * math.log2(math.e)
    for g in range(group):
        q_all[g * rows : (g + 1) * rows, :] = q_ref[:, g * head_size : (g + 1) * head_size]
    m_ref[...] = jnp.full(m_ref.shape, masked_score, jnp.float32)
    l_ref[...] = jnp.zeros(l_ref.shape, jnp.float32)
    acc_ref[...] = jnp.zeros(acc_ref.shape, jnp.float32)

    def step(start, masked):
        k = k_ref[0, start : start + tile, :]
        v = v_ref[0, start : start + tile, :]
        s = lax.dot_general(
            q_all[...], k, (((1,), (1,)), ((), ())), preferred_element_type=jnp.float32
        ) * factor
        if masked:
            token = lax.broadcasted_iota(jnp.int32, (rows, tile), 0)
            slot = lax.broadcasted_iota(jnp.int32, (rows, tile), 1) + start
            seen = (slot < live) & (slot < edge + token)
            seen = jnp.concatenate([seen] * group, axis=0)
            s = jnp.where(seen, s, masked_score)
        m_old = m_ref[:, :1]
        m_new = jnp.maximum(m_old, jnp.max(s, axis=1, keepdims=True))
        p = jnp.exp2(s - m_new)
        if masked:
            p = jnp.where(seen, p, 0.0)
        shrink = jnp.exp2(m_old - m_new)
        l_new = l_ref[:, :1] * shrink + jnp.sum(p, axis=1, keepdims=True)
        acc_ref[...] = acc_ref[...] * shrink + jnp.dot(
            p.astype(jnp.bfloat16), v, preferred_element_type=jnp.float32
        )
        m_ref[...] = jnp.broadcast_to(m_new, m_ref.shape)
        l_ref[...] = jnp.broadcast_to(l_new, l_ref.shape)

    for start in range(0, keys, tile):
        whole = (start + tile <= live) & (start + tile <= edge)
        some = (start < live) & (start < edge + rows - 1)

        @pl.when(whole)
        def _():
            step(start, False)

        @pl.when(some & jnp.logical_not(whole))
        def _():
            step(start, True)

    total = l_ref[:, :1]
    held = jnp.where(total > 0.0, total, 1.0)
    out = acc_ref[...] / held
    stat = jnp.where(total > 0.0, m_ref[:, :1] + jnp.log2(held), masked_score)

    @pl.when(kv == 0)
    def _():
        s_ref[...] = jnp.full(s_ref.shape, masked_score, jnp.float32)

    lane = lax.broadcasted_iota(jnp.int32, s_ref.shape, 1)
    stats = s_ref[...]
    for g in range(group):
        o_ref[:, g * head_size : (g + 1) * head_size] = out[g * rows : (g + 1) * rows].astype(o_ref.dtype)
        stats = jnp.where(lane == kv * group + g, stat[g * rows : (g + 1) * rows], stats)
    s_ref[...] = stats


def attend(q, keys, values, bounds, group, tile):
    rows, width = q.shape
    kv_local, key_count, head_size = keys.shape
    wide = group * head_size
    return pl.pallas_call(
        functools.partial(attend_kernel, tile, group, head_size),
        out_shape=(
            jax.ShapeDtypeStruct((rows, width), jnp.bfloat16),
            jax.ShapeDtypeStruct((rows, LANES), jnp.float32),
        ),
        grid_spec=pltpu.PrefetchScalarGridSpec(
            num_scalar_prefetch=1,
            grid=(kv_local,),
            in_specs=[
                pl.BlockSpec((rows, wide), lambda i, b: (0, i)),
                pl.BlockSpec((1, key_count, head_size), lambda i, b: (i, 0, 0)),
                pl.BlockSpec((1, key_count, head_size), lambda i, b: (i, 0, 0)),
            ],
            out_specs=[
                pl.BlockSpec((rows, wide), lambda i, b: (0, i)),
                pl.BlockSpec((rows, LANES), lambda i, b: (0, 0)),
            ],
            scratch_shapes=[
                pltpu.VMEM((group * rows, head_size), jnp.bfloat16),
                pltpu.VMEM((group * rows, LANES), jnp.float32),
                pltpu.VMEM((group * rows, LANES), jnp.float32),
                pltpu.VMEM((group * rows, head_size), jnp.float32),
            ],
        ),
        compiler_params=pltpu.CompilerParams(vmem_limit_bytes=48 << 20),
        cost_estimate=pl.CostEstimate(
            flops=4 * rows * width * key_count,
            bytes_accessed=4 * rows * width + 4 * keys.size,
            transcendentals=rows * (width // head_size) * key_count,
        ),
    )(bounds, q, keys, values)


def merge_kernel(head_size, *refs):
    parts = len(refs) // 2
    outs, stats, final = refs[:parts], refs[parts : 2 * parts], refs[-1]
    joined = functools.reduce(jnp.maximum, [s[...] for s in stats])
    weights = [jnp.exp2(s[...] - joined) for s in stats]
    inverse = 1.0 / functools.reduce(jnp.add, weights)
    weights = [w * inverse for w in weights]
    for h in range(final.shape[1] // head_size):
        cols = slice(h * head_size, (h + 1) * head_size)
        total = functools.reduce(
            jnp.add,
            [o[:, cols].astype(jnp.float32) * w[:, h : h + 1] for o, w in zip(outs, weights)],
        )
        final[:, cols] = total.astype(final.dtype)


def merge(outs, stats, head_size):
    return pl.pallas_call(
        functools.partial(merge_kernel, head_size),
        out_shape=jax.ShapeDtypeStruct(outs[0].shape, jnp.bfloat16),
    )(*outs, *stats)


def on_device(queries, prefix_keys, cached_prefix_values, shard_len, reach, w_out):
    shard_count = lax.axis_size("blk")
    own_index = lax.axis_index("blk")
    rows, heads_local, head_size = queries.shape
    kv_local, keys_len = prefix_keys.shape[:2]
    group = heads_local // kv_local
    tile = min(1024, keys_len)
    q = queries.reshape(rows, heads_local * head_size)
    live = shard_len[own_index]

    visitors = [q] + [passed_along(q, "blk", offset) for offset in range(1, SPAN)]
    outs, stats = [], []
    for offset in range(SPAN):
        owner = (own_index - offset + shard_count) % shard_count
        bounds = jnp.stack([live, reach[owner] - offset * keys_len]).astype(jnp.int32)
        out, stat = attend(visitors[offset], prefix_keys, cached_prefix_values, bounds, group, tile)
        if offset:
            out, stat = passed_along((out, stat), "blk", -offset)
        outs.append(out)
        stats.append(stat)
    attended = merge(outs, stats, head_size)
    gathered = lax.all_gather(attended, "blk", axis=0, tiled=True)
    splits = lax.axis_size("heads")
    me = lax.axis_index("heads")
    size = gathered.shape[0] // splits

    def share(owner):
        return jnp.dot(
            lax.dynamic_slice_in_dim(gathered, owner * size, size, 0),
            w_out,
            preferred_element_type=jnp.float32,
        )

    received = []
    for step in range(1, splits):
        sent = share((me + step) % splits).astype(jnp.bfloat16)
        received.append(passed_along(sent, "heads", step))
    total = share(me)
    for piece in received:
        total = total + piece.astype(jnp.float32)
    return total.astype(jnp.bfloat16)


def solution(mesh):
    return jax.shard_map(
        on_device,
        mesh=mesh,
        in_specs=(
            P("blk", "heads", None),
            P("heads", "blk", None),
            P("heads", "blk", None),
            P(),
            P(),
            P("heads", "blk"),
        ),
        out_specs=P("heads", "blk"),
        check_vma=False,
    )
```

time: 339 us -> 241 us (0.71)
  matrix products: 79.7 us -> 19.3 us
  waiting for transfers between devices: 167 us -> 121 us
  other arithmetic: 43.7 us -> 3.67 us
  Pallas kernels: 0 us -> 35.1 us
  starting transfers between devices: 18.4 us -> 35 us
  local copies, waits for them, and re-layouts: 13.3 us -> 9.79 us
    dot_general x9 -> x2, matrix products: 79.7 us -> 19.3 us  [share(): jnp.dot(lax.dynamic_slice_in_dim(gathered, owner * size, size, 0), w_out,...]
    reduce_scatter x1 -> x0, waiting for transfers between devices: 53.3 us -> none  [on_device(): lax.psum_scatter(partial_out, 'heads', scatter_dimension=0, tiled=True)]
    pallas_call x0 -> x5, Pallas kernels: none -> 35.1 us  [the longest x4 31.4 us: attend(): pl.pallas_call(functools.partial(attend_kernel, tile, group, head_size),...]
    reduce_sum x4 -> x0, other arithmetic: 32.5 us -> none  [part_stats(): totals = jnp.sum(weights, axis=-1)]
    ppermute x12 -> x10, starting transfers between devices: 18.3 us -> 35 us  [passed_along(): return lax.ppermute(value, axis, pairs)]
    convert_element_type x2 -> x0, other arithmetic: 6.93 us -> none  [the longest x1 4.21 us: on_device(): attended = (running[2] / running[1][..., None]).astype(jnp.bfloat16).resh...]
    exp x6 -> x0, local copies, waits for them, and re-layouts: 6.07 us -> none  [the longest x3 3.04 us: combine_parts(): second_factor = jnp.exp(second[0] - joined)]
    ppermute x12 -> x10, waiting for transfers between devices: 29.3 us -> 33.9 us  [passed_along(): return lax.ppermute(value, axis, pairs)]
  transfers between devices with their start and end apart: 14 -> 11, of which waited for: 4 -> 4; matrix products, arithmetic and copies ran while one was open for 33% -> 3% of each run, Pallas kernels for 0% -> 13%
where the time goes in v1:
time: 241 us; the launch traced here: 239 us
  waiting for transfers between devices  121 us (50%)
  Pallas kernels  35.1 us (15%)
  starting transfers between devices  35 us (15%)
  matrix products  19.3 us (8%)
  between operations  15.5 us (6%)
  local copies, waits for them, and re-layouts  9.79 us (4%)
  other arithmetic  3.67 us (2%)
    all_gather x1, waiting for transfers between devices, on_device(): gathered = lax.all_gather(attended, 'blk', axis=0, tiled=True)  86.9 us
    ppermute x10, starting transfers between devices, passed_along(): return lax.ppermute(value, axis, pairs)  35 us
    ppermute x10, waiting for transfers between devices, passed_along(): return lax.ppermute(value, axis, pairs)  33.9 us
    pallas_call x4, Pallas kernels, attend(): pl.pallas_call(functools.partial(attend_kernel, tile, group, head_size),...  31.4 us
    dot_general x2, matrix products, share(): jnp.dot(lax.dynamic_slice_in_dim(gathered, owner * size, size, 0), w_out,...  19.3 us
    unnamed x23, local copies, waits for them, and re-layouts  6.99 us
  transfers between devices with their start and end apart: 11, of which 4 were waited for; matrix products, arithmetic and copies ran while one was open for 3% of the time, Pallas kernels for 13%

profile of v1, /device:TPU:14, one launch (start us, length us, event | category | flops | bytes accessed | tf_op | source)
XLA Modules:
  0.0 239.1 jit_solution(7416011868876210735)
XLA Ops:
  6.5 1.3 copy.9
  7.8 1.0 collective-permute-start.4
  8.8 1.5 collective-permute-start.2
  10.3 0.5 collective-permute-start
  10.8 1.3 dynamic_slice.21
  12.1 1.5 fusion.11
  14.8 0.8 pad_add_fusion.3.bounds
  15.6 0.8 pad_add_fusion.1.bounds
  17.1 0.8 pad_add_fusion.2.bounds
  17.8 4.2 %collective-permute-done.4.q_ref = bf16[64,4096]{1,0:T(8,128)(2,1)S(1)} collective-permute-done((bf16[64,4096]{1,0:T(8,128)(2,1)S(1)}, bf16[64,4096]{1,0:T(8,128)(2,1)S(1)}, u32[]{:S(2)}, u32[]{:S(2)}) %collective-permute-start.4) | collective-permute-done | bytes 524320 | tf_op jit(solution)/shard_map/ppermute | solution.py:19
  22.1 1.6 copy-done.2
  23.7 1.6 copy-done.4
  25.2 2.1 shard_map.67
  27.6 4.9 %collective-permute-done.2.q_ref = bf16[64,4096]{1,0:T(8,128)(2,1)S(1)} collective-permute-done((bf16[64,4096]{1,0:T(8,128)(2,1)S(1)}, bf16[64,4096]{1,0:T(8,128)(2,1)S(1)}, u32[]{:S(2)}, u32[]{:S(2)}) %collective-permute-start.2) | collective-permute-done | bytes 524320 | tf_op jit(solution)/shard_map/ppermute | solution.py:19
  32.5 9.7 %shard_map.66 = (bf16[64,4096]{1,0:T(8,128)(2,1)S(1)}, f32[64,128]{1,0:T(8,128)S(1)}) custom-call(s32[2]{0:T(128)S(1)} %pad_add_fusion.2.bounds, bf16[64,4096]{1,0:T(8,128)(2,1)S(1)} %collective-permute-done.2.q_ref, bf16[4,2048,128]{2,1,0:T(8,128)(2,1)S(1)} %copy-done.2, bf16[4,2048,128]{2,1,0:T(8,128)(2,1)S(1)} %copy-done.4), custom_call_target="tpu_custom_call" | custom-call | flops 2147483648 | bytes 5242880 | tf_op jit(solution)/shard_map/pallas_call | solution.py:92
  42.2 6.5 %collective-permute-start.3 = (bf16[64,4096]{1,0:T(8,128)(2,1)S(1)}, bf16[64,4096]{1,0:T(8,128)(2,1)S(1)}, u32[]{:S(2)}, u32[]{:S(2)}) collective-permute-start(bf16[64,4096]{1,0:T(8,128)(2,1)S(1)} %get-tuple-element.15), channel_id=1, source_target_pairs={{0,14},{1,15},{2,0},{3,1},{4,2},{5,3},{6,4},{7,5},{8,6},{9,7},{10,... | collective-permute-start | bytes 1572872 | tf_op jit(solution)/shard_map/ppermute | solution.py:19
  48.7 9.7 %shard_map.65 = (bf16[64,4096]{1,0:T(8,128)(2,1)S(1)}, f32[64,128]{1,0:T(8,128)S(1)}) custom-call(s32[2]{0:T(128)S(1)} %pad_add_fusion.1.bounds, bf16[64,4096]{1,0:T(8,128)(2,1)S(1)} %collective-permute-done.q_ref, bf16[4,2048,128]{2,1,0:T(8,128)(2,1)S(1)} %copy-done.2, bf16[4,2048,128]{2,1,0:T(8,128)(2,1)S(1)} %copy-done.4), custom_call_target="tpu_custom_call" | custom-call | flops 2147483648 | bytes 5242880 | tf_op jit(solution)/shard_map/pallas_call | solution.py:92
  58.4 2.6 %collective-permute-start.1 = (bf16[64,4096]{1,0:T(8,128)(2,1)S(1)}, bf16[64,4096]{1,0:T(8,128)(2,1)S(1)}, u32[]{:S(2)}, u32[]{:S(2)}) collective-permute-start(bf16[64,4096]{1,0:T(8,128)(2,1)S(1)} %get-tuple-element.14), channel_id=1, source_target_pairs={{0,15},{1,0},{2,1},{3,2},{4,3},{5,4},{6,5},{7,6},{8,7},{9,8},{10,9... | collective-permute-start | bytes 1572872 | tf_op jit(solution)/shard_map/ppermute | solution.py:19
  61.0 13.8 %collective-permute-start.8 = (f32[64,128]{1,0:T(8,128)S(1)}, f32[64,128]{1,0:T(8,128)S(1)}, u32[]{:S(2)}, u32[]{:S(2)}) collective-permute-start(f32[64,128]{1,0:T(8,128)S(1)} %get-tuple-element.20), channel_id=1, source_target_pairs={{0,13},{1,14},{2,15},{3,0},{4,1},{5,2},{6,3},{7,4},{8,5},{9,6},{10... | collective-permute-start | bytes 98312 | tf_op jit(solution)/shard_map/ppermute | solution.py:19
  74.8 1.4 pad_add_fusion.bounds
  76.2 7.4 %collective-permute-start.7 = (f32[64,128]{1,0:T(8,128)S(1)}, f32[64,128]{1,0:T(8,128)S(1)}, u32[]{:S(2)}, u32[]{:S(2)}) collective-permute-start(f32[64,128]{1,0:T(8,128)S(1)} %get-tuple-element.19), channel_id=1, source_target_pairs={{0,14},{1,15},{2,0},{3,1},{4,2},{5,3},{6,4},{7,5},{8,6},{9,7},{10,... | collective-permute-start | bytes 98312 | tf_op jit(solution)/shard_map/ppermute | solution.py:19
  83.6 0.9 collective-permute-start.6
  84.5 10.0 %shard_map.64 = (bf16[64,4096]{1,0:T(8,128)(2,1)S(1)}, f32[64,128]{1,0:T(8,128)S(1)}) custom-call(s32[2]{0:T(128)S(1)} %pad_add_fusion.bounds, bf16[64,4096]{1,0:T(8,128)(2,1)S(1)} %bitcast.9, bf16[4,2048,128]{2,1,0:T(8,128)(2,1)S(1)} %copy-done.3, bf16[4,2048,128]{2,1,0:T(8,128)(2,1)S(1)} %copy-done.4), custom_call_target="tpu_custom_call" | custom-call | flops 2147483648 | bytes 5242880 | tf_op jit(solution)/shard_map/pallas_call | solution.py:92
  94.5 0.8 copy-done
  95.2 0.6 copy-done.1
  95.9 0.5 copy-done.9
  97.1 3.6 %shard_map.68 = bf16[64,4096]{1,0:T(8,128)(2,1)} custom-call(bf16[64,4096]{1,0:T(8,128)(2,1)} %copy-done, bf16[64,4096]{1,0:T(8,128)(2,1)} %copy-done.7, bf16[64,4096]{1,0:T(8,128)(2,1)} %copy-done.6, bf16[64,4096]{1,0:T(8,128)(2,1)} %copy-done.5, f32[64,128]{1,0:T(8,128)} %copy-done.1, f32[64,128]{1,0:T(8,128)} %copy-done.10, f32[64,128]{1,0:T(8,128)} %copy-done.9, ...), custom_call_target="tpu_custom_call" | custom-call | tf_op jit(solution)/shard_map/pallas_call | solution.py:143
  100.8 86.9 %all-gather.2.cloned.1.call-done = bf16[1024,4096]{1,0:T(8,128)(2,1)} async-done(((bf16[64,4096]{1,0:T(8,128)(2,1)}), bf16[1024,4096]{1,0:T(8,128)(2,1)}) %all-gather.2.cloned.1.call-update) | async-done | bytes 8388624 | tf_op jit(solution)/shard_map/all_gather | solution.py:170
  187.6 9.1 %fusion.6 = bf16[512,1024]{1,0:T(8,128)(2,1)S(1)} fusion(bf16[4096,1024]{1,0:T(8,128)(2,1)} %param.11, bf16[1024,4096]{1,0:T(8,128)(2,1)} %all-gather.2.cloned.1.call-done, s32[]{:T(128)S(6)} %select_n.55), kind=kOutput, calls=%fused_computation.5 | convolution fusion | flops 4295491584 | bytes 13631492 | tf_op jit(solution)/shard_map/dot_general | solution.py:176
  196.8 0.6 collective-permute-start.9
  197.4 24.8 %collective-permute-done.9 = bf16[512,1024]{1,0:T(8,128)(2,1)S(1)} collective-permute-done((bf16[512,1024]{1,0:T(8,128)(2,1)S(1)}, bf16[512,1024]{1,0:T(8,128)(2,1)S(1)}, u32[]{:S(2)}, u32[]{:S(2)}) %collective-permute-start.9) | collective-permute-done | bytes 1048608 | tf_op jit(solution)/shard_map/ppermute | solution.py:19
  222.2 10.1 %add_convert_fusion = bf16[512,1024]{1,0:T(8,128)(2,1)} fusion(bf16[512,1024]{1,0:T(8,128)(2,1)S(1)} %collective-permute-done.9, bf16[4096,1024]{1,0:T(8,128)(2,1)} %param.11, bf16[1024,4096]{1,0:T(8,128)(2,1)} %all-gather.2.cloned.1.call-done, s32[]{:T(128)S(6)} %select_n.53), kind=kOutput, calls=%fused_computation.4 | convolution fusion | flops 4296540160 | bytes 14680068 | tf_op jit(solution)/shard_map/dot_general | solution.py:176
  (27 shorter events, 0.9 us)
Async XLA Ops:
  6.5 181.1 %all-gather.2.cloned.1.call-start = ((), (), s32[]{:S(2)}) async-start(), calls=%async_computation | async-start | bytes 8912896 | tf_op jit(solution)/shard_map/all_gather | solution.py:170
  7.8 14.3 %collective-permute-start.4 = (bf16[64,4096]{1,0:T(8,128)(2,1)S(1)}, bf16[64,4096]{1,0:T(8,128)(2,1)S(1)}, u32[]{:S(2)}, u32[]{:S(2)}) collective-permute-start(bf16[64,4096]{1,0:T(8,128)(2,1)S(1)} %bitcast.6), channel_id=1, source_target_pairs={{0,3},{1,4},{2,5},{3,6},{4,7},{5,8},{6,9},{7,10},{8,11},{9,12},{10... | collective-permute-start | bytes 1572872 | tf_op jit(solution)/shard_map/ppermute | solution.py:19
  8.8 23.7 %collective-permute-start.2 = (bf16[64,4096]{1,0:T(8,128)(2,1)S(1)}, bf16[64,4096]{1,0:T(8,128)(2,1)S(1)}, u32[]{:S(2)}, u32[]{:S(2)}) collective-permute-start(bf16[64,4096]{1,0:T(8,128)(2,1)S(1)} %bitcast.7), channel_id=1, source_target_pairs={{0,2},{1,3},{2,4},{3,5},{4,6},{5,7},{6,8},{7,9},{8,10},{9,11},{10,... | collective-permute-start | bytes 1572872 | tf_op jit(solution)/shard_map/ppermute | solution.py:19
  10.3 38.3 %collective-permute-start = (bf16[64,4096]{1,0:T(8,128)(2,1)S(1)}, bf16[64,4096]{1,0:T(8,128)(2,1)S(1)}, u32[]{:S(2)}, u32[]{:S(2)}) collective-permute-start(bf16[64,4096]{1,0:T(8,128)(2,1)S(1)} %bitcast.8), channel_id=1, source_target_pairs={{0,1},{1,2},{2,3},{3,4},{4,5},{5,6},{6,7},{7,8},{8,9},{9,10},{10,1... | collective-permute-start | bytes 1572872 | tf_op jit(solution)/shard_map/ppermute | solution.py:19
  22.1 1.6 copy-start.2
  23.7 1.6 copy-start.4
  27.3 57.1 %copy-start.3 = (bf16[4,2048,128]{2,1,0:T(8,128)(2,1)S(1)}, bf16[4,2048,128]{2,1,0:T(8,128)(2,1)}, u32[]{:S(2)}) copy-start(bf16[4,2048,128]{2,1,0:T(8,128)(2,1)} %k_ref.7) | copy-start | bytes 6291460
  27.3 68.5 %collective-permute-start.5 = (bf16[64,4096]{1,0:T(8,128)(2,1)S(1)}, bf16[64,4096]{1,0:T(8,128)(2,1)S(1)}, u32[]{:S(2)}, u32[]{:S(2)}) collective-permute-start(bf16[64,4096]{1,0:T(8,128)(2,1)S(1)} %get-tuple-element.16), channel_id=1, source_target_pairs={{0,13},{1,14},{2,15},{3,0},{4,1},{5,2},{6,3},{7,4},{8,5},{9,6},{10... | collective-permute-start | bytes 1572872 | tf_op jit(solution)/shard_map/ppermute | solution.py:19
  42.2 53.7 %collective-permute-start.3 = (bf16[64,4096]{1,0:T(8,128)(2,1)S(1)}, bf16[64,4096]{1,0:T(8,128)(2,1)S(1)}, u32[]{:S(2)}, u32[]{:S(2)}) collective-permute-start(bf16[64,4096]{1,0:T(8,128)(2,1)S(1)} %get-tuple-element.15), channel_id=1, source_target_pairs={{0,14},{1,15},{2,0},{3,1},{4,2},{5,3},{6,4},{7,5},{8,6},{9,7},{10,... | collective-permute-start | bytes 1572872 | tf_op jit(solution)/shard_map/ppermute | solution.py:19
  58.4 37.6 %collective-permute-start.1 = (bf16[64,4096]{1,0:T(8,128)(2,1)S(1)}, bf16[64,4096]{1,0:T(8,128)(2,1)S(1)}, u32[]{:S(2)}, u32[]{:S(2)}) collective-permute-start(bf16[64,4096]{1,0:T(8,128)(2,1)S(1)} %get-tuple-element.14), channel_id=1, source_target_pairs={{0,15},{1,0},{2,1},{3,2},{4,3},{5,4},{6,5},{7,6},{8,7},{9,8},{10,9... | collective-permute-start | bytes 1572872 | tf_op jit(solution)/shard_map/ppermute | solution.py:19
  61.0 22.6 %collective-permute-start.8 = (f32[64,128]{1,0:T(8,128)S(1)}, f32[64,128]{1,0:T(8,128)S(1)}, u32[]{:S(2)}, u32[]{:S(2)}) collective-permute-start(f32[64,128]{1,0:T(8,128)S(1)} %get-tuple-element.20), channel_id=1, source_target_pairs={{0,13},{1,14},{2,15},{3,0},{4,1},{5,2},{6,3},{7,4},{8,5},{9,6},{10... | collective-permute-start | bytes 98312 | tf_op jit(solution)/shard_map/ppermute | solution.py:19
  76.2 19.7 %collective-permute-start.7 = (f32[64,128]{1,0:T(8,128)S(1)}, f32[64,128]{1,0:T(8,128)S(1)}, u32[]{:S(2)}, u32[]{:S(2)}) collective-permute-start(f32[64,128]{1,0:T(8,128)S(1)} %get-tuple-element.19), channel_id=1, source_target_pairs={{0,14},{1,15},{2,0},{3,1},{4,2},{5,3},{6,4},{7,5},{8,6},{9,7},{10,... | collective-permute-start | bytes 98312 | tf_op jit(solution)/shard_map/ppermute | solution.py:19
  83.6 12.3 %copy-start.8 = (f32[64,128]{1,0:T(8,128)}, f32[64,128]{1,0:T(8,128)S(1)}, u32[]{:S(2)}) copy-start(f32[64,128]{1,0:T(8,128)S(1)} %collective-permute-done.8.refs_7_) | copy-start | bytes 98308
  83.6 12.3 %collective-permute-start.6 = (f32[64,128]{1,0:T(8,128)S(1)}, f32[64,128]{1,0:T(8,128)S(1)}, u32[]{:S(2)}, u32[]{:S(2)}) collective-permute-start(f32[64,128]{1,0:T(8,128)S(1)} %get-tuple-element.18), channel_id=1, source_target_pairs={{0,15},{1,0},{2,1},{3,2},{4,3},{5,4},{6,5},{7,6},{8,7},{9,8},{10,9... | collective-permute-start | bytes 98312 | tf_op jit(solution)/shard_map/ppermute | solution.py:19
  94.4 0.8 copy-start
  95.2 0.6 copy-start.1
  95.9 0.6 copy-start.9
  95.9 0.6 copy-start.10
  95.9 0.8 copy-start.5
  95.9 1.0 copy-start.6
  95.9 1.2 copy-start.7
  196.8 25.4 %collective-permute-start.9 = (bf16[512,1024]{1,0:T(8,128)(2,1)S(1)}, bf16[512,1024]{1,0:T(8,128)(2,1)S(1)}, u32[]{:S(2)}, u32[]{:S(2)}) collective-permute-start(bf16[512,1024]{1,0:T(8,128)(2,1)S(1)} %fusion.6), channel_id=1, source_target_pairs={{0,16},{16,0},{1,17},{17,1},{2,18},{18,2},{3,19},{19,3},{4,20},{20... | collective-permute-start | bytes 3145736 | tf_op jit(solution)/shard_map/ppermute | solution.py:19
Sparse Core Ops, SparseCore 0:
  100.9 86.7 all-gather.1

commit v2 on v1

--- a/solution.py
+++ b/solution.py
@@ -146,6 +146,200 @@
     )(*outs, *stats)
 
 
+def project_kernel(row_sets, chunks, a_ref, w_ref, o_ref, buf, w_buf, acc, outgoing, incoming,
+                   local_sem, col_send, col_recv, pair_send, pair_recv, core_send, core_recv, share_send, share_recv):
+    splits = lax.axis_size("heads")
+    h = lax.axis_index("heads")
+    me = lax.axis_index("blk")
+    r, p, c = me // 4, (me // 2) % 2, me % 2
+    rows, width = a_ref.shape
+    wide = width // chunks
+    band = 4 * rows
+    per_share = row_sets // splits
+    columns = w_ref.shape[1]
+    strip = min(256, columns)
+    first = ((h + 1) % splits) * per_share
+
+    def block(row_set, pair, core):
+        return (row_set * 2 + pair) * 2 + core
+
+    def view(index, chunk):
+        return buf.at[chunk, pl.ds(pl.multiple_of(index * rows, rows), rows), :]
+
+    def own(chunk):
+        return a_ref.at[:, pl.ds(pl.multiple_of(chunk * wide, wide), wide)]
+
+    def remote(src, dst, sent, landed, head, blk):
+        return pltpu.make_async_remote_copy(
+            src_ref=src, dst_ref=dst, send_sem=sent, recv_sem=landed,
+            device_id=(head, blk), device_id_type=pl.DeviceIdType.MESH,
+        )
+
+    def to_column(d, chunk, row_set):
+        return remote(own(chunk), view(block(row_set, p, c), chunk), col_send.at[(d - 1) * chunks + chunk],
+                      col_recv.at[row_set * chunks + chunk], h, block((r + d) % row_sets, p, c))
+
+    def to_pair(src, row_set, pair, chunk):
+        at = row_set * chunks + chunk
+        return remote(src, view(block(row_set, pair, c), chunk), pair_send.at[at], pair_recv.at[at], h, block(r, 1 - p, c))
+
+    def to_core(src, row_set, pair, core, chunk):
+        at = (pair * row_sets + row_set) * chunks + chunk
+        return remote(src, view(block(row_set, pair, core), chunk), core_send.at[at], core_recv.at[at], h, block(r, p, 1 - c))
+
+    def to_share(k):
+        row_set = (first + k) % row_sets
+        owner = row_set // per_share
+        slot = ((h - owner + splits) % splits - 1) * per_share + row_set % per_share
+        return remote(outgoing.at[k], incoming.at[slot], share_send.at[k], share_recv.at[slot], owner, me)
+
+    def from_share(slot):
+        return remote(outgoing.at[0], incoming.at[slot], share_send.at[0], share_recv.at[slot], (h + 1) % splits, me)
+
+    barrier = pltpu.get_barrier_semaphore()
+    greeted = [(h, block((r + d) % row_sets, p, c)) for d in range(1, row_sets)]
+    greeted += [(h, block(r, 1 - p, c)), (h, block(r, p, 1 - c))]
+    greeted += [((h + d) % splits, me) for d in range(1, splits)]
+    w_copy = pltpu.make_async_copy(w_ref, w_buf, local_sem.at[chunks])
+    w_copy.start()
+    kept = [pltpu.make_async_copy(own(ch), view(me, ch), local_sem.at[ch]) for ch in range(chunks)]
+    for copy in kept:
+        copy.start()
+    for peer in greeted:
+        pl.semaphore_signal(barrier, inc=1, device_id=peer, device_id_type=pl.DeviceIdType.MESH)
+    pl.semaphore_wait(barrier, len(greeted))
+
+    for ch in range(chunks):
+        for d in range(1, row_sets):
+            to_column(d, ch, r).start()
+        to_pair(own(ch), r, p, ch).start()
+        to_core(own(ch), r, p, c, ch).start()
+    for copy in kept:
+        copy.wait()
+    w_copy.wait()
+
+    total = row_sets * chunks
+
+    def located(t):
+        k = t // chunks
+        return k, t % chunks, (first + k) % row_sets
+
+    def step(s, carry):
+        @pl.when(s < total)
+        def _():
+            k, ch, row_set = located(s)
+
+            @pl.when(row_set != r)
+            def _():
+                to_column(1, ch, row_set).wait_recv()
+                to_pair(view(block(row_set, p, c), ch), row_set, p, ch).start()
+                to_core(view(block(row_set, p, c), ch), row_set, p, c, ch).start()
+
+        @pl.when((s >= 1) & (s <= total))
+        def _():
+            k, ch, row_set = located(s - 1)
+            to_pair(view(block(row_set, 1 - p, c), ch), row_set, 1 - p, ch).wait_recv()
+            to_core(view(block(row_set, 1 - p, c), ch), row_set, 1 - p, c, ch).start()
+
+        @pl.when(s >= 2)
+        def _():
+            k, ch, row_set = located(s - 2)
+            for pair in range(2):
+                to_core(view(block(row_set, pair, 1 - c), ch), row_set, pair, 1 - c, ch).wait_recv()
+            at = pl.multiple_of(row_set * band, band)
+
+            def multiply(n, carry):
+                cols = pl.ds(pl.multiple_of(n * strip, strip), strip)
+                value = jnp.dot(
+                    buf[ch, pl.ds(at, band), :],
+                    w_buf[pl.ds(pl.multiple_of(ch * wide, wide), wide), cols],
+                    preferred_element_type=jnp.float32,
+                )
+
+                @pl.when(ch == 0)
+                def _():
+                    acc[:, cols] = value
+
+                @pl.when(ch > 0)
+                def _():
+                    acc[:, cols] += value
+
+                return carry
+
+            lax.fori_loop(0, columns // strip, multiply, 0)
+
+            @pl.when((ch == chunks - 1) & (k < row_sets - per_share))
+            def _():
+                outgoing[k] = acc[...].astype(outgoing.dtype)
+                to_share(k).start()
+
+            @pl.when((ch == chunks - 1) & (k >= row_sets - per_share))
+            def _():
+                j = row_set % per_share
+                value = acc[...]
+                for d in range(splits - 1):
+                    from_share(d * per_share + j).wait_recv()
+                    value = value + incoming[d * per_share + j].astype(jnp.float32)
+                o_ref[pl.ds(pl.multiple_of(j * band, band), band), :] = value.astype(o_ref.dtype)
+
+        return carry
+
+    lax.fori_loop(0, total + 2, step, 0)
+
+    def drain(t, carry):
+        k, ch, row_set = located(t)
+        to_pair(view(me, ch), row_set, p, ch).wait_send()
+        for pair in range(2):
+            to_core(view(me, ch), row_set, pair, c, ch).wait_send()
+        return carry
+
+    lax.fori_loop(0, total, drain, 0)
+    for ch in range(chunks):
+        for d in range(1, row_sets):
+            to_column(d, ch, r).wait_send()
+
+    def drain_share(k, carry):
+        to_share(k).wait_send()
+        return carry
+
+    lax.fori_loop(0, row_sets - per_share, drain_share, 0)
+
+
+def project(attended, w_out, chunks):
+    count, splits = lax.axis_size("blk"), lax.axis_size("heads")
+    rows, width = attended.shape
+    columns = w_out.shape[1]
+    row_sets = count // 4
+    per_share = row_sets // splits
+    band = 4 * rows
+    dma = pltpu.SemaphoreType.DMA
+    return pl.pallas_call(
+        functools.partial(project_kernel, row_sets, chunks),
+        out_shape=jax.ShapeDtypeStruct((per_share * band, columns), jnp.bfloat16),
+        in_specs=[pl.BlockSpec(memory_space=pl.ANY)] * 2,
+        out_specs=pl.BlockSpec(memory_space=pltpu.VMEM),
+        scratch_shapes=[
+            pltpu.VMEM((chunks, count * rows, width // chunks), jnp.bfloat16),
+            pltpu.VMEM(w_out.shape, jnp.bfloat16),
+            pltpu.VMEM((band, columns), jnp.float32),
+            pltpu.VMEM((row_sets - per_share, band, columns), jnp.bfloat16),
+            pltpu.VMEM((row_sets - per_share, band, columns), jnp.bfloat16),
+            dma((chunks + 1,)),
+            dma(((row_sets - 1) * chunks,)),
+            dma((row_sets * chunks,)),
+            dma((row_sets * chunks,)),
+            dma((row_sets * chunks,)),
+            dma((2 * row_sets * chunks,)),
+            dma((2 * row_sets * chunks,)),
+            dma((row_sets - per_share,)),
+            dma((row_sets - per_share,)),
+        ],
+        compiler_params=pltpu.CompilerParams(
+            collective_id=0, has_side_effects=True, vmem_limit_bytes=48 << 20
+        ),
+    )(attended, w_out)
+
+
 def on_device(queries, prefix_keys, cached_prefix_values, shard_len, reach, w_out):
     shard_count = lax.axis_size("blk")
     own_index = lax.axis_index("blk")
@@ -167,26 +361,7 @@
         outs.append(out)
         stats.append(stat)
     attended = merge(outs, stats, head_size)
-    gathered = lax.all_gather(attended, "blk", axis=0, tiled=True)
-    splits = lax.axis_size("heads")
-    me = lax.axis_index("heads")
-    size = gathered.shape[0] // splits
-
-    def share(owner):
-        return jnp.dot(
-            lax.dynamic_slice_in_dim(gathered, owner * size, size, 0),
-            w_out,
-            preferred_element_type=jnp.float32,
-        )
-
-    received = []
-    for step in range(1, splits):
-        sent = share((me + step) % splits).astype(jnp.bfloat16)
-        received.append(passed_along(sent, "heads", step))
-    total = share(me)
-    for piece in received:
-        total = total + piece.astype(jnp.float32)
-    return total.astype(jnp.bfloat16)
+    return project(attended, w_out, 2)
 
 
 def solution(mesh):

time: 241 us -> 193 us (0.80)
  the two profiles are of different devices: /device:TPU:14 before, /device:TPU:9 now
where the time goes in v2:
time: 193 us; the launch traced here: 192 us
  Pallas kernels  133 us (69%)
  starting transfers between devices  39.1 us (20%)
  local copies, waits for them, and re-layouts  11.8 us (6%)
  other arithmetic  3.67 us (2%)
  waiting for transfers between devices  2.55 us (1%)
  between operations  2.05 us (1%)
    pallas_call x1, Pallas kernels, project(): pl.pallas_call(functools.partial(project_kernel, row_sets, chunks), out_s...  98.5 us
    ppermute x9, starting transfers between devices, passed_along(): return lax.ppermute(value, axis, pairs)  39.1 us
    pallas_call x4, Pallas kernels, attend(): pl.pallas_call(functools.partial(attend_kernel, tile, group, head_size),...  31.1 us
    unnamed x26, local copies, waits for them, and re-layouts  8.98 us
  transfers between devices with their start and end apart: 9, of which 1 were waited for; matrix products, arithmetic and copies ran while one was open for 3% of the time, Pallas kernels for 16%

profile of v2, /device:TPU:9, one launch (start us, length us, event | category | flops | bytes accessed | tf_op | source)
XLA Modules:
  0.0 192.3 jit_solution(2629817791599177785)
XLA Ops:
  0.0 1.3 copy.9
  1.3 1.9 collective-permute-start
  3.1 1.2 collective-permute-start.2
  4.3 0.4 collective-permute-start.4
  4.7 1.5 fusion
  6.9 1.3 dynamic_slice.15
  8.8 0.7 pad_add_fusion.1.bounds
  9.5 0.7 pad_add_fusion.2.bounds
  10.9 0.7 pad_add_fusion.3.bounds
  11.7 2.5 %collective-permute-done.q_ref = bf16[64,4096]{1,0:T(8,128)(2,1)S(1)} collective-permute-done((bf16[64,4096]{1,0:T(8,128)(2,1)S(1)}, bf16[64,4096]{1,0:T(8,128)(2,1)S(1)}, u32[]{:S(2)}, u32[]{:S(2)}) %collective-permute-start) | collective-permute-done | bytes 524320 | tf_op jit(solution)/shard_map/ppermute | solution.py:19
  14.2 1.6 copy-done.3
  15.8 1.6 copy-done.5
  17.4 9.7 %shard_map.65 = (bf16[64,4096]{1,0:T(8,128)(2,1)S(1)}, f32[64,128]{1,0:T(8,128)S(1)}) custom-call(s32[2]{0:T(128)S(1)} %pad_add_fusion.1.bounds, bf16[64,4096]{1,0:T(8,128)(2,1)S(1)} %collective-permute-done.q_ref, bf16[4,2048,128]{2,1,0:T(8,128)(2,1)S(1)} %copy-done.3, bf16[4,2048,128]{2,1,0:T(8,128)(2,1)S(1)} %copy-done.5), custom_call_target="tpu_custom_call" | custom-call | flops 2147483648 | bytes 5242880 | tf_op jit(solution)/shard_map/pallas_call | solution.py:92
  27.1 10.0 %collective-permute-start.1 = (bf16[64,4096]{1,0:T(8,128)(2,1)S(1)}, bf16[64,4096]{1,0:T(8,128)(2,1)S(1)}, u32[]{:S(2)}, u32[]{:S(2)}) collective-permute-start(bf16[64,4096]{1,0:T(8,128)(2,1)S(1)} %get-tuple-element.14), channel_id=1, source_target_pairs={{0,15},{1,0},{2,1},{3,2},{4,3},{5,4},{6,5},{7,6},{8,7},{9,8},{10,9... | collective-permute-start | bytes 1572872 | tf_op jit(solution)/shard_map/ppermute | solution.py:19
  37.0 9.7 %shard_map.66 = (bf16[64,4096]{1,0:T(8,128)(2,1)S(1)}, f32[64,128]{1,0:T(8,128)S(1)}) custom-call(s32[2]{0:T(128)S(1)} %pad_add_fusion.2.bounds, bf16[64,4096]{1,0:T(8,128)(2,1)S(1)} %collective-permute-done.2.q_ref, bf16[4,2048,128]{2,1,0:T(8,128)(2,1)S(1)} %copy-done.3, bf16[4,2048,128]{2,1,0:T(8,128)(2,1)S(1)} %copy-done.5), custom_call_target="tpu_custom_call" | custom-call | flops 2147483648 | bytes 5242880 | tf_op jit(solution)/shard_map/pallas_call | solution.py:92
  46.7 0.5 collective-permute-start.3
  47.2 2.1 %shard_map.67 = (bf16[64,4096]{1,0:T(8,128)(2,1)S(1)}, f32[64,128]{1,0:T(8,128)S(1)}) custom-call(s32[2]{0:T(128)S(1)} %pad_add_fusion.3.bounds, bf16[64,4096]{1,0:T(8,128)(2,1)S(1)} %collective-permute-done.4.q_ref, bf16[4,2048,128]{2,1,0:T(8,128)(2,1)S(1)} %copy-done.3, bf16[4,2048,128]{2,1,0:T(8,128)(2,1)S(1)} %copy-done.5), custom_call_target="tpu_custom_call" | custom-call | flops 2147483648 | bytes 5242880 | tf_op jit(solution)/shard_map/pallas_call | solution.py:92
  49.3 17.5 %collective-permute-start.5 = (bf16[64,4096]{1,0:T(8,128)(2,1)S(1)}, bf16[64,4096]{1,0:T(8,128)(2,1)S(1)}, u32[]{:S(2)}, u32[]{:S(2)}) collective-permute-start(bf16[64,4096]{1,0:T(8,128)(2,1)S(1)} %get-tuple-element.16), channel_id=1, source_target_pairs={{0,13},{1,14},{2,15},{3,0},{4,1},{5,2},{6,3},{7,4},{8,5},{9,6},{10... | collective-permute-start | bytes 1572872 | tf_op jit(solution)/shard_map/ppermute | solution.py:19
  66.8 1.3 collective-permute-start.6
  68.2 1.4 pad_add_fusion.bounds
  69.6 5.9 %collective-permute-start.7 = (f32[64,128]{1,0:T(8,128)S(1)}, f32[64,128]{1,0:T(8,128)S(1)}, u32[]{:S(2)}, u32[]{:S(2)}) collective-permute-start(f32[64,128]{1,0:T(8,128)S(1)} %get-tuple-element.19), channel_id=1, source_target_pairs={{0,14},{1,15},{2,0},{3,1},{4,2},{5,3},{6,4},{7,5},{8,6},{9,7},{10,... | collective-permute-start | bytes 98312 | tf_op jit(solution)/shard_map/ppermute | solution.py:19
  75.5 0.4 collective-permute-start.8
  75.9 9.7 %shard_map.64 = (bf16[64,4096]{1,0:T(8,128)(2,1)S(1)}, f32[64,128]{1,0:T(8,128)S(1)}) custom-call(s32[2]{0:T(128)S(1)} %pad_add_fusion.bounds, bf16[64,4096]{1,0:T(8,128)(2,1)S(1)} %bitcast.7, bf16[4,2048,128]{2,1,0:T(8,128)(2,1)S(1)} %copy-done.4, bf16[4,2048,128]{2,1,0:T(8,128)(2,1)S(1)} %copy-done.5), custom_call_target="tpu_custom_call" | custom-call | flops 2147483648 | bytes 5242880 | tf_op jit(solution)/shard_map/pallas_call | solution.py:92
  85.6 0.8 copy-done.1
  86.4 0.6 copy-done.2
  87.1 0.5 copy-done.10
  87.6 0.2 copy-done.6
  87.8 0.2 copy-done.7
  88.2 3.6 %shard_map.68.a_ref = bf16[64,4096]{1,0:T(8,128)(2,1)} custom-call(bf16[64,4096]{1,0:T(8,128)(2,1)} %copy-done.1, bf16[64,4096]{1,0:T(8,128)(2,1)} %copy-done.6, bf16[64,4096]{1,0:T(8,128)(2,1)} %copy-done.7, bf16[64,4096]{1,0:T(8,128)(2,1)} %copy-done.8, f32[64,128]{1,0:T(8,128)} %copy-done.2, f32[64,128]{1,0:T(8,128)} %copy-done.9, f32[64,128]{1,0:T(8,128)} %copy-done.10, ...), custom_call_target="tpu_custom_call" | custom-call | tf_op jit(solution)/shard_map/pallas_call | solution.py:143
  91.8 1.0 copy-done
  92.8 98.5 %shard_map.69 = bf16[512,1024]{1,0:T(8,128)(2,1)S(1)} custom-call(bf16[64,4096]{1,0:T(8,128)(2,1)S(1)} %copy-done, bf16[4096,1024]{1,0:T(8,128)(2,1)} %w_ref.1), custom_call_target="tpu_custom_call" | custom-call | tf_op jit(solution)/shard_map/pallas_call | solution.py:316
  191.3 1.0 copy.11
  (24 shorter events, 0.2 us)
Async XLA Ops:
  1.3 13.0 %collective-permute-start = (bf16[64,4096]{1,0:T(8,128)(2,1)S(1)}, bf16[64,4096]{1,0:T(8,128)(2,1)S(1)}, u32[]{:S(2)}, u32[]{:S(2)}) collective-permute-start(bf16[64,4096]{1,0:T(8,128)(2,1)S(1)} %bitcast.4), channel_id=1, source_target_pairs={{0,1},{1,2},{2,3},{3,4},{4,5},{5,6},{6,7},{7,8},{8,9},{9,10},{10,1... | collective-permute-start | bytes 1572872 | tf_op jit(solution)/shard_map/ppermute | solution.py:19
  3.1 33.9 %collective-permute-start.2 = (bf16[64,4096]{1,0:T(8,128)(2,1)S(1)}, bf16[64,4096]{1,0:T(8,128)(2,1)S(1)}, u32[]{:S(2)}, u32[]{:S(2)}) collective-permute-start(bf16[64,4096]{1,0:T(8,128)(2,1)S(1)} %bitcast.5), channel_id=1, source_target_pairs={{0,2},{1,3},{2,4},{3,5},{4,6},{5,7},{6,8},{7,9},{8,10},{9,11},{10,... | collective-permute-start | bytes 1572872 | tf_op jit(solution)/shard_map/ppermute | solution.py:19
  4.3 42.9 %collective-permute-start.4 = (bf16[64,4096]{1,0:T(8,128)(2,1)S(1)}, bf16[64,4096]{1,0:T(8,128)(2,1)S(1)}, u32[]{:S(2)}, u32[]{:S(2)}) collective-permute-start(bf16[64,4096]{1,0:T(8,128)(2,1)S(1)} %bitcast.6), channel_id=1, source_target_pairs={{0,3},{1,4},{2,5},{3,6},{4,7},{5,8},{6,9},{7,10},{8,11},{9,12},{10... | collective-permute-start | bytes 1572872 | tf_op jit(solution)/shard_map/ppermute | solution.py:19
  14.2 1.6 copy-start.3
  15.8 1.6 copy-start.5
  27.1 59.9 %collective-permute-start.1 = (bf16[64,4096]{1,0:T(8,128)(2,1)S(1)}, bf16[64,4096]{1,0:T(8,128)(2,1)S(1)}, u32[]{:S(2)}, u32[]{:S(2)}) collective-permute-start(bf16[64,4096]{1,0:T(8,128)(2,1)S(1)} %get-tuple-element.14), channel_id=1, source_target_pairs={{0,15},{1,0},{2,1},{3,2},{4,3},{5,4},{6,5},{7,6},{8,7},{9,8},{10,9... | collective-permute-start | bytes 1572872 | tf_op jit(solution)/shard_map/ppermute | solution.py:19
  46.7 29.1 %copy-start.4 = (bf16[4,2048,128]{2,1,0:T(8,128)(2,1)S(1)}, bf16[4,2048,128]{2,1,0:T(8,128)(2,1)}, u32[]{:S(2)}) copy-start(bf16[4,2048,128]{2,1,0:T(8,128)(2,1)} %k_ref.7) | copy-start | bytes 6291460
  46.7 40.3 %collective-permute-start.3 = (bf16[64,4096]{1,0:T(8,128)(2,1)S(1)}, bf16[64,4096]{1,0:T(8,128)(2,1)S(1)}, u32[]{:S(2)}, u32[]{:S(2)}) collective-permute-start(bf16[64,4096]{1,0:T(8,128)(2,1)S(1)} %get-tuple-element.15), channel_id=1, source_target_pairs={{0,14},{1,15},{2,0},{3,1},{4,2},{5,3},{6,4},{7,5},{8,6},{9,7},{10,... | collective-permute-start | bytes 1572872 | tf_op jit(solution)/shard_map/ppermute | solution.py:19
  49.3 37.7 %collective-permute-start.5 = (bf16[64,4096]{1,0:T(8,128)(2,1)S(1)}, bf16[64,4096]{1,0:T(8,128)(2,1)S(1)}, u32[]{:S(2)}, u32[]{:S(2)}) collective-permute-start(bf16[64,4096]{1,0:T(8,128)(2,1)S(1)} %get-tuple-element.16), channel_id=1, source_target_pairs={{0,13},{1,14},{2,15},{3,0},{4,1},{5,2},{6,3},{7,4},{8,5},{9,6},{10... | collective-permute-start | bytes 1572872 | tf_op jit(solution)/shard_map/ppermute | solution.py:19
  66.8 8.7 %collective-permute-start.6 = (f32[64,128]{1,0:T(8,128)S(1)}, f32[64,128]{1,0:T(8,128)S(1)}, u32[]{:S(2)}, u32[]{:S(2)}) collective-permute-start(f32[64,128]{1,0:T(8,128)S(1)} %get-tuple-element.18), channel_id=1, source_target_pairs={{0,15},{1,0},{2,1},{3,2},{4,3},{5,4},{6,5},{7,6},{8,7},{9,8},{10,9... | collective-permute-start | bytes 98312 | tf_op jit(solution)/shard_map/ppermute | solution.py:19
  69.6 17.4 %collective-permute-start.7 = (f32[64,128]{1,0:T(8,128)S(1)}, f32[64,128]{1,0:T(8,128)S(1)}, u32[]{:S(2)}, u32[]{:S(2)}) collective-permute-start(f32[64,128]{1,0:T(8,128)S(1)} %get-tuple-element.19), channel_id=1, source_target_pairs={{0,14},{1,15},{2,0},{3,1},{4,2},{5,3},{6,4},{7,5},{8,6},{9,7},{10,... | collective-permute-start | bytes 98312 | tf_op jit(solution)/shard_map/ppermute | solution.py:19
  75.5 10.1 %copy-start.9 = (f32[64,128]{1,0:T(8,128)}, f32[64,128]{1,0:T(8,128)S(1)}, u32[]{:S(2)}) copy-start(f32[64,128]{1,0:T(8,128)S(1)} %collective-permute-done.6.refs_5_) | copy-start | bytes 98308
  75.5 11.5 %collective-permute-start.8 = (f32[64,128]{1,0:T(8,128)S(1)}, f32[64,128]{1,0:T(8,128)S(1)}, u32[]{:S(2)}, u32[]{:S(2)}) collective-permute-start(f32[64,128]{1,0:T(8,128)S(1)} %get-tuple-element.20), channel_id=1, source_target_pairs={{0,13},{1,14},{2,15},{3,0},{4,1},{5,2},{6,3},{7,4},{8,5},{9,6},{10... | collective-permute-start | bytes 98312 | tf_op jit(solution)/shard_map/ppermute | solution.py:19
  85.6 0.8 copy-start.1
  86.4 0.6 copy-start.2
  87.0 0.6 copy-start.10
  87.0 0.6 copy-start.11
  87.0 0.8 copy-start.6
  87.0 1.0 copy-start.7
  87.1 1.1 copy-start.8
  91.8 1.0 copy-start

commit v3 on v0

v3 whole, which is shorter than its diff:
```python
import functools
import math

import jax
import jax.numpy as jnp
from jax import lax
from jax.experimental import pallas as pl
from jax.experimental.pallas import tpu as pltpu
from jax.sharding import PartitionSpec as P

SPAN = 4
masked_score = -1e30


def layer_kernel(row_sets, chunks, rows, q_ref, k_ref, v_ref, live_ref, reach_ref, w_ref, o_ref,
                 q_all, k_all, v_all, part_own, stat_own, part_out, stat_out, part_in, stat_in,
                 buf, w_buf, acc, outgoing, incoming,
                 local_sem, q_send, q_recv, part_send, part_recv, stat_send, stat_recv,
                 col_send, col_recv, pair_send, pair_recv, core_send, core_recv, share_send, share_recv):
    splits = lax.axis_size("heads")
    count = lax.axis_size("blk")
    h = lax.axis_index("heads")
    me = lax.axis_index("blk")
    r, p, c = me // 4, (me // 2) % 2, me % 2
    kv_local, lanes, head_size = q_ref.shape
    group = lanes // rows
    keys = k_ref.shape[1]
    per_chunk = kv_local // chunks
    wide = per_chunk * group * head_size
    band = 4 * rows
    per_share = row_sets // splits
    columns = w_ref.shape[1]
    strip = min(256, columns)
    first = ((h + 1) % splits) * per_share
    visits = SPAN - 1

    def block(row_set, pair, core):
        return (row_set * 2 + pair) * 2 + core

    def view(index, chunk):
        return buf.at[chunk, pl.ds(pl.multiple_of(index * rows, rows), rows), :]

    def remote(src, dst, sent, landed, head, blk):
        return pltpu.make_async_remote_copy(
            src_ref=src, dst_ref=dst, send_sem=sent, recv_sem=landed,
            device_id=(head, blk), device_id_type=pl.DeviceIdType.MESH,
        )

    def heads_of(chunk):
        return pl.ds(chunk * per_chunk, per_chunk)

    def to_visit(offset, chunk):
        at = (offset - 1) * chunks + chunk
        return remote(q_ref.at[heads_of(chunk)], q_all.at[offset, heads_of(chunk)], q_send.at[at], q_recv.at[at],
                      h, (me + offset) % count)

    def part_home(offset, chunk):
        at = (offset - 1) * chunks + chunk
        return remote(part_out.at[offset - 1, heads_of(chunk)], part_in.at[offset - 1, heads_of(chunk)],
                      part_send.at[at], part_recv.at[at], h, (me - offset + count) % count)

    def stat_home(offset, chunk):
        at = (offset - 1) * chunks + chunk
        return remote(stat_out.at[offset - 1, heads_of(chunk)], stat_in.at[offset - 1, heads_of(chunk)],
                      stat_send.at[at], stat_recv.at[at], h, (me - offset + count) % count)

    def to_column(d, chunk, row_set):
        return remote(view(me, chunk), view(block(row_set, p, c), chunk), col_send.at[(d - 1) * chunks + chunk],
                      col_recv.at[row_set * chunks + chunk], h, block((r + d) % row_sets, p, c))

    def to_pair(row_set, pair, chunk):
        at = row_set * chunks + chunk
        spot = view(block(row_set, pair, c), chunk)
        return remote(spot, spot, pair_send.at[at], pair_recv.at[at], h, block(r, 1 - p, c))

    def to_core(row_set, pair, core, chunk):
        at = (pair * row_sets + row_set) * chunks + chunk
        spot = view(block(row_set, pair, core), chunk)
        return remote(spot, spot, core_send.at[at], core_recv.at[at], h, block(r, p, 1 - c))

    def to_share(k):
        row_set = (first + k) % row_sets
        owner = row_set // per_share
        slot = ((h - owner + splits) % splits - 1) * per_share + row_set % per_share
        return remote(outgoing.at[k], incoming.at[slot], share_send.at[k], share_recv.at[slot], owner, me)

    def from_share(slot):
        return remote(outgoing.at[0], incoming.at[slot], share_send.at[0], share_recv.at[slot], (h + 1) % splits, me)

    q_copy = pltpu.make_async_copy(q_ref, q_all.at[0], local_sem.at[0])
    k_copy = pltpu.make_async_copy(k_ref, k_all, local_sem.at[1])
    v_copy = pltpu.make_async_copy(v_ref, v_all, local_sem.at[2])
    w_copy = pltpu.make_async_copy(w_ref, w_buf, local_sem.at[3])
    for copy in (q_copy, k_copy, v_copy, w_copy):
        copy.start()
    greeted = [(h, block((r + d) % row_sets, p, c)) for d in range(1, row_sets)]
    greeted += [(h, block(r, 1 - p, c)), (h, block(r, p, 1 - c))]
    greeted += [((h + d) % splits, me) for d in range(1, splits)]
    for d in range(1, SPAN):
        greeted += [(h, (me + d) % count), (h, (me - d + count) % count)]
    barrier = pltpu.get_barrier_semaphore()
    for peer in greeted:
        pl.semaphore_signal(barrier, inc=1, device_id=peer, device_id_type=pl.DeviceIdType.MESH)
    pl.semaphore_wait(barrier, len(greeted))
    for ch in range(chunks):
        for offset in range(1, SPAN):
            to_visit(offset, ch).start()
    q_copy.wait()
    k_copy.wait()
    v_copy.wait()

    live = live_ref[me]
    factor = head_size**-0.5 * math.log2(math.e)
    sub = min(256, lanes)

    def attend(offset, chunk):
        edge = reach_ref[(me - offset + count) % count] - offset * keys
        token = lax.broadcasted_iota(jnp.int32, (1, sub), 1) % rows
        limit = jnp.minimum(edge + token, live)
        slot = lax.broadcasted_iota(jnp.int32, (keys, sub), 0)
        seen = slot < limit

        def one(i, carry):
            kv = chunk * per_chunk + i
            key_tile, value_tile = k_all[kv], v_all[kv]
            for start in range(0, lanes, sub):
                cols = slice(start, start + sub)
                s = lax.dot_general(
                    key_tile, q_all[offset, kv, cols, :], (((1,), (1,)), ((), ())),
                    preferred_element_type=jnp.float32,
                )
                s = jnp.where(seen, s * factor, masked_score)
                m = jnp.max(s, axis=0, keepdims=True)
                weight = jnp.exp2(s - m)
                total = jnp.sum(weight, axis=0, keepdims=True)
                part = lax.dot_general(
                    value_tile, weight.astype(jnp.bfloat16), (((0,), (0,)), ((), ())),
                    preferred_element_type=jnp.float32,
                )
                part = (part * (1.0 / total)).astype(jnp.bfloat16)
                stat = jnp.broadcast_to(m + jnp.log2(total), (8, sub))

                @pl.when(offset == 0)
                def _():
                    part_own[kv, :, cols] = part
                    stat_own[kv, :, cols] = stat

                @pl.when(offset > 0)
                def _():
                    part_out[offset - 1, kv, :, cols] = part
                    stat_out[offset - 1, kv, :, cols] = stat

            return carry

        lax.fori_loop(0, per_chunk, one, 0)

    def merge(chunk):
        for offset in range(1, SPAN):
            part_home(offset, chunk).wait_recv()
            stat_home(offset, chunk).wait_recv()
        spot = pl.ds(pl.multiple_of(me * rows, rows), rows)
        for i in range(per_chunk):
            kv = chunk * per_chunk + i
            stats = [stat_own[kv, :1, :]] + [stat_in[j, kv, :1, :] for j in range(visits)]
            joined = functools.reduce(jnp.maximum, stats)
            weights = [jnp.exp2(s - joined) for s in stats]
            inverse = 1.0 / functools.reduce(jnp.add, weights)
            parts = [part_own[kv]] + [part_in[j, kv] for j in range(visits)]
            total = functools.reduce(
                jnp.add, [x.astype(jnp.float32) * (w * inverse) for x, w in zip(parts, weights)]
            )
            total = total.T.astype(jnp.bfloat16)
            for g in range(group):
                at = (i * group + g) * head_size
                buf[chunk, spot, at : at + head_size] = total[g * rows : (g + 1) * rows]
        for d in range(1, row_sets):
            to_column(d, chunk, r).start()
        to_pair(r, p, chunk).start()
        to_core(r, p, c, chunk).start()

    def relay(row_set, chunk):
        @pl.when(row_set != r)
        def _():
            to_column(1, chunk, row_set).wait_recv()
            to_pair(row_set, p, chunk).start()
            to_core(row_set, p, c, chunk).start()

    def unit(u, carry):
        early = u < chunks
        offset = jnp.where(early, 0, (u - chunks) % visits + 1)
        chunk = jnp.where(early, u, (u - chunks) // visits)

        @pl.when(offset > 0)
        def _():
            to_visit(offset, chunk).wait_recv()

        attend(offset, chunk)

        @pl.when(offset > 0)
        def _():
            part_home(offset, chunk).start()
            stat_home(offset, chunk).start()

        for ch in range(chunks - 1):
            @pl.when(u == chunks + visits * (ch + 1))
            def _():
                merge(ch)

        return carry

    lax.fori_loop(0, SPAN * chunks, unit, 0)

    def relay_early(t, carry):
        relay((first + t % row_sets) % row_sets, t // row_sets)
        return carry

    lax.fori_loop(0, row_sets * (chunks - 1), relay_early, 0)
    merge(chunks - 1)
    w_copy.wait()

    total = row_sets * chunks

    def located(t):
        k = t % row_sets
        return k, t // row_sets, (first + k) % row_sets

    def step(s, carry):
        @pl.when((s < total) & (s >= total - row_sets))
        def _():
            k, ch, row_set = located(s)
            relay(row_set, ch)

        @pl.when((s >= 1) & (s <= total))
        def _():
            k, ch, row_set = located(s - 1)
            to_pair(row_set, 1 - p, ch).wait_recv()
            to_core(row_set, 1 - p, c, ch).start()

        @pl.when(s >= 2)
        def _():
            k, ch, row_set = located(s - 2)
            for pair in range(2):
                to_core(row_set, pair, 1 - c, ch).wait_recv()
            at = pl.multiple_of(row_set * band, band)

            def multiply(n, carry):
                cols = pl.ds(pl.multiple_of(n * strip, strip), strip)
                value = jnp.dot(
                    buf[ch, pl.ds(at, band), :],
                    w_buf[pl.ds(pl.multiple_of(ch * wide, wide), wide), cols],
                    preferred_element_type=jnp.float32,
                )

                @pl.when(ch == 0)
                def _():
                    acc[k, :, cols] = value

                @pl.when(ch > 0)
                def _():
                    acc[k, :, cols] += value

                return carry

            lax.fori_loop(0, columns // strip, multiply, 0)

            @pl.when((ch == chunks - 1) & (k < row_sets - per_share))
            def _():
                outgoing[k] = acc[k].astype(outgoing.dtype)
                to_share(k).start()

            @pl.when((ch == chunks - 1) & (k >= row_sets - per_share))
            def _():
                j = row_set % per_share
                value = acc[k]
                for d in range(splits - 1):
                    from_share(d * per_share + j).wait_recv()
                    value = value + incoming[d * per_share + j].astype(jnp.float32)
                o_ref[pl.ds(pl.multiple_of(j * band, band), band), :] = value.astype(o_ref.dtype)

        return carry

    lax.fori_loop(0, total + 2, step, 0)

    for ch in range(chunks):
        for offset in range(1, SPAN):
            to_visit(offset, ch).wait_send()
            part_home(offset, ch).wait_send()
            stat_home(offset, ch).wait_send()
        for d in range(1, row_sets):
            to_column(d, ch, r).wait_send()

    def drain(t, carry):
        k, ch, row_set = located(t)
        to_pair(row_set, p, ch).wait_send()
        for pair in range(2):
            to_core(row_set, pair, c, ch).wait_send()
        return carry

    lax.fori_loop(0, total, drain, 0)

    def drain_share(k, carry):
        to_share(k).wait_send()
        return carry

    lax.fori_loop(0, row_sets - per_share, drain_share, 0)


def on_device(queries, prefix_keys, cached_prefix_values, shard_len, reach, w_out):
    count, splits = lax.axis_size("blk"), lax.axis_size("heads")
    rows, heads_local, head_size = queries.shape
    kv_local, keys_len = prefix_keys.shape[:2]
    group = heads_local // kv_local
    lanes = group * rows
    chunks = 2 if kv_local % 2 == 0 else 1
    columns = w_out.shape[1]
    row_sets = count // 4
    per_share = row_sets // splits
    band = 4 * rows
    visits = SPAN - 1
    q = queries.reshape(rows, kv_local, group, head_size).transpose(1, 2, 0, 3).reshape(kv_local, lanes, head_size)
    dma = pltpu.SemaphoreType.DMA
    bf16, f32 = jnp.bfloat16, jnp.float32
    anywhere = pl.BlockSpec(memory_space=pl.ANY)
    scalars = pl.BlockSpec(memory_space=pltpu.SMEM)
    each = dma((visits * chunks,))
    sets = dma((row_sets * chunks,))
    return pl.pallas_call(
        functools.partial(layer_kernel, row_sets, chunks, rows),
        out_shape=jax.ShapeDtypeStruct((per_share * band, columns), bf16),
        in_specs=[anywhere, anywhere, anywhere, scalars, scalars, anywhere],
        out_specs=pl.BlockSpec(memory_space=pltpu.VMEM),
        scratch_shapes=[
            pltpu.VMEM((SPAN, kv_local, lanes, head_size), bf16),
            pltpu.VMEM(prefix_keys.shape, bf16),
            pltpu.VMEM(prefix_keys.shape, bf16),
            pltpu.VMEM((kv_local, head_size, lanes), bf16),
            pltpu.VMEM((kv_local, 8, lanes), f32),
            pltpu.VMEM((visits, kv_local, head_size, lanes), bf16),
            pltpu.VMEM((visits, kv_local, 8, lanes), f32),
            pltpu.VMEM((visits, kv_local, head_size, lanes), bf16),
            pltpu.VMEM((visits, kv_local, 8, lanes), f32),
            pltpu.VMEM((chunks, count * rows, heads_local * head_size // chunks), bf16),
            pltpu.VMEM(w_out.shape, bf16),
            pltpu.VMEM((row_sets, band, columns), f32),
            pltpu.VMEM((row_sets - per_share, band, columns), bf16),
            pltpu.VMEM((row_sets - per_share, band, columns), bf16),
            dma((4,)),
            each, each, each, each, each, each,
            dma(((row_sets - 1) * chunks,)),
            sets, sets, sets,
            dma((2 * row_sets * chunks,)),
            dma((2 * row_sets * chunks,)),
            dma((row_sets - per_share,)),
            dma((row_sets - per_share,)),
        ],
        compiler_params=pltpu.CompilerParams(
            collective_id=0, has_side_effects=True, vmem_limit_bytes=60 << 20
        ),
    )(q, prefix_keys, cached_prefix_values, shard_len, reach, w_out)


def solution(mesh):
    return jax.shard_map(
        on_device,
        mesh=mesh,
        in_specs=(
            P("blk", "heads", None),
            P("heads", "blk", None),
            P("heads", "blk", None),
            P(),
            P(),
            P("heads", "blk"),
        ),
        out_specs=P("heads", "blk"),
        check_vma=False,
    )
```

time: 339 us -> 147 us (0.43); the launches traced: 335 us -> 147 us
  waiting for transfers between devices: 167 us -> 0 us
  Pallas kernels: 0 us -> 143 us
  matrix products: 79.7 us -> 0 us
  other arithmetic: 43.7 us -> 0 us
  starting transfers between devices: 18.4 us -> 0 us
  between operations: 13.6 us -> 0.01 us
  local copies, waits for them, and re-layouts: 13.3 us -> 4.3 us
    pallas_call x0 -> x1, Pallas kernels: none -> 143 us  [on_device(): pl.pallas_call(functools.partial(layer_kernel, row_sets, chunks, rows), o...]
    all_gather x1 -> x0, waiting for transfers between devices: 84.2 us -> none  [on_device(): lax.all_gather(attended, 'blk', axis=0, tiled=True)]
    dot_general x9 -> x0, matrix products: 79.7 us -> none  [the longest x4 33.5 us: part_stats(): jnp.einsum('thgn,hnd->thgd', weights.astype(jnp.bfloat16), value_block, p...]
    reduce_scatter x1 -> x0, waiting for transfers between devices: 53.3 us -> none  [on_device(): lax.psum_scatter(partial_out, 'heads', scatter_dimension=0, tiled=True)]
    reduce_sum x4 -> x0, other arithmetic: 32.5 us -> none  [part_stats(): totals = jnp.sum(weights, axis=-1)]
    ppermute x12 -> x0, waiting for transfers between devices: 29.3 us -> none  [passed_along(): return lax.ppermute(value, axis, pairs)]
    ppermute x12 -> x0, starting transfers between devices: 18.3 us -> none  [passed_along(): return lax.ppermute(value, axis, pairs)]
    convert_element_type x2 -> x0, other arithmetic: 6.93 us -> none  [the longest x1 4.21 us: on_device(): attended = (running[2] / running[1][..., None]).astype(jnp.bfloat16).resh...]
  transfers between devices with their start and end apart: 14 -> 0, of which waited for: 4 -> 0; matrix products, arithmetic and copies ran while one was open for 33% -> 0% of each run, Pallas kernels for 0% -> 0%
where the time goes in v3:
time: 147 us
  Pallas kernels  143 us (97%)
  local copies, waits for them, and re-layouts  4.3 us (3%)
    pallas_call x1, Pallas kernels, on_device(): pl.pallas_call(functools.partial(layer_kernel, row_sets, chunks, rows), o...  143 us

profile of v3, /device:TPU:14, one launch (start us, length us, event | category | flops | bytes accessed | tf_op | source)
XLA Modules:
  0.0 147.0 jit_solution(15296546102907970649)
XLA Ops:
  0.0 2.0 %copy.7 = bf16[64,4,8,128]{3,0,2,1:T(8,128)(2,1)} copy(bf16[64,4,8,128]{3,2,1,0:T(8,128)(2,1)} %bitcast.5) | data formatting | bytes 1048576 | tf_op jit(solution)/shard_map/reshape | solution.py:320
  2.0 142.7 %shard_map.64 = bf16[512,1024]{1,0:T(8,128)(2,1)} custom-call(bf16[4,512,128]{2,1,0:T(8,128)(2,1)} %bitcast.4, bf16[4,2048,128]{2,1,0:T(8,128)(2,1)} %k_ref.1, bf16[4,2048,128]{2,1,0:T(8,128)(2,1)} %v_ref.1, s32[16]{0:T(128)} %live_ref.1, s32[16]{0:T(128)} %reach_ref.1, bf16[4096,1024]{1,0:T(8,128)(2,1)} %w_ref.1), custom_call_target="tpu_custom_call" | custom-call | tf_op jit(solution)/shard_map/pallas_call | solution.py:327
  144.7 2.3 %copy.9 = bf16[512,1024]{1,0:T(8,128)(2,1)} copy(bf16[512,1024]{1,0:T(8,128)(2,1)} %shard_map.64) | data formatting | bytes 2097152

commit v4 on v3

--- a/solution.py
+++ b/solution.py
@@ -111,7 +111,7 @@
 
     live = live_ref[me]
     factor = head_size**-0.5 * math.log2(math.e)
-    sub = min(256, lanes)
+    sub = min(512, lanes)
 
     def attend(offset, chunk):
         edge = reach_ref[(me - offset + count) % count] - offset * keys

time: 147 us -> 140 us (0.952)
  Pallas kernels: 143 us -> 135 us
    pallas_call x1, Pallas kernels: 143 us -> 135 us  [on_device(): pl.pallas_call(functools.partial(layer_kernel, row_sets, chunks, rows), o...]
where the time goes in v4:
time: 140 us
  Pallas kernels  135 us (96%)
  local copies, waits for them, and re-layouts  4.3 us (3%)
    pallas_call x1, Pallas kernels, on_device(): pl.pallas_call(functools.partial(layer_kernel, row_sets, chunks, rows), o...  135 us

profile of v4, /device:TPU:14, one launch (start us, length us, event | category | flops | bytes accessed | tf_op | source)
XLA Modules:
  0.0 139.8 jit_solution(13669808539833648615)
XLA Ops:
  0.0 2.0 %copy.7 = bf16[64,4,8,128]{3,0,2,1:T(8,128)(2,1)} copy(bf16[64,4,8,128]{3,2,1,0:T(8,128)(2,1)} %bitcast.5) | data formatting | bytes 1048576 | tf_op jit(solution)/shard_map/reshape | solution.py:320
  2.0 135.5 %shard_map.64 = bf16[512,1024]{1,0:T(8,128)(2,1)} custom-call(bf16[4,512,128]{2,1,0:T(8,128)(2,1)} %bitcast.4, bf16[4,2048,128]{2,1,0:T(8,128)(2,1)} %k_ref.1, bf16[4,2048,128]{2,1,0:T(8,128)(2,1)} %v_ref.1, s32[16]{0:T(128)} %live_ref.1, s32[16]{0:T(128)} %reach_ref.1, bf16[4096,1024]{1,0:T(8,128)(2,1)} %w_ref.1), custom_call_target="tpu_custom_call" | custom-call | tf_op jit(solution)/shard_map/pallas_call | solution.py:327
  137.5 2.3 %copy.9 = bf16[512,1024]{1,0:T(8,128)(2,1)} copy(bf16[512,1024]{1,0:T(8,128)(2,1)} %shard_map.64) | data formatting | bytes 2097152
